TPU v7x, 32 devices: a whole 2x2x4 slice. The times are simulated.
32 devices in a mesh: group: 2 (over x), expert: 16 (over z, y, core).
Axes of the slice: x: 2, y: 2, z: 4, core: 2. Of those that a mesh axis runs over, the one named last changes fastest.
Arguments:
- tokens: bfloat16 [4096, 3584], P(('group', 'expert')), parts along dimension 0, may hold values from -6 to 6
- routes: int32 [4096, 1], P(('group', 'expert')), parts along dimension 0, may hold values from 0 to 3; in each aligned block of 128 rows (0 to 127, 128 to 255, ...) at most 64 rows name the same one
- gate_weights: float32 [4096, 1], P(('group', 'expert')), parts along dimension 0, may hold values from 0.25 to 1
- w_gate: bfloat16 [16, 3584, 512], P('expert'), may hold values from -0.09375 to 0.09375
- w_up: bfloat16 [16, 3584, 512], P('expert'), may hold values from -0.09375 to 0.09375
- w_down: bfloat16 [16, 512, 3584], P('expert'), may hold values from -0.125 to 0.125
Outputs:
- layer_out: bfloat16 [4096, 3584], P(('group', 'expert')), parts along dimension 0
There are 2 independent parts, one for each index of `group`. A program takes and returns all parts, laid end to end along the dimension named above; an argument that names none is the same for every part. Nothing has to cross between parts.
Inputs may be any that keep to these rules, and one draw needn't show every extreme that they name: `routes`: each token names one of the 4 experts; among the 128 tokens of one device no expert is named more than 64 times, and in every draw some device names some expert exactly 64 times.
All inputs are finite; a program needn't handle non-finite values.
Results may differ from a plain program's by a relative error of at most 0.0085.
Values may be sent and summed in bfloat16 or wider, within the bound.
No kernel may reach another device: no remote copies, remote signals or barrier semaphores. Data moves between devices by JAX's collectives and lax.ppermute only.
A program may use at most 128 MiB of HBM per device.

v0:
```python
import functools

import jax
import jax.numpy as jnp
from jax import lax
from jax.experimental import pallas as pl
from jax.experimental.pallas import tpu as pltpu
from jax.sharding import Mesh
from jax.sharding import PartitionSpec as P


SPAN = 4
SWAP = [(0, 1), (1, 0)]
VMEM = pl.BlockSpec(memory_space=pltpu.VMEM)
SMEM = pl.BlockSpec(memory_space=pltpu.SMEM)
HBM = pl.BlockSpec(memory_space=pltpu.HBM)


def held(x):
    return pltpu.with_memory_space_constraint(x, pltpu.HBM)


def tile_of(size, most):
    return max(t for t in range(128, most + 1, 128) if size % t == 0)


def steps_to(route, plane, experts):
    if experts & (experts - 1) == 0:
        return route ^ plane
    return lax.rem(route - plane + experts, experts)


def grids(rows):
    return [lax.broadcasted_iota(jnp.int32, (rows, rows), d) for d in range(2)]


def turned(row):
    rows = row.shape[1]
    sub, lane = grids(rows)
    wide = jnp.broadcast_to(row, (rows, rows))
    return jnp.sum(jnp.where(sub == lane, wide, jnp.zeros_like(wide)), axis=1, keepdims=True)


def slots_by_row(row, plane, experts, capacity):
    sub, lane = grids(row.shape[1])
    before = ((turned(row) == row) & (sub < lane)).astype(jnp.int32)
    position = jnp.sum(before, axis=0, keepdims=True)
    return steps_to(row, plane, experts) * capacity + position


def pack_kernel(experts, capacity, plane_ref, routes_ref, tokens_ref, *refs):
    outs, (routes, tokens, sems) = refs[:-3], refs[-3:]
    rows, width = tokens.shape
    half = width // 2
    first = pltpu.make_async_copy(routes_ref, routes, sems.at[2])
    first.start()
    copies = []
    for c in range(2):
        part = pl.ds(c * half, half)
        copies.append(
            pltpu.make_async_copy(tokens_ref.at[:, part], tokens.at[:, part], sems.at[c])
        )
        copies[c].start()
    first.wait()
    slot = slots_by_row(routes[...], plane_ref[0], experts, capacity)
    every = lax.broadcasted_iota(jnp.int32, (experts * capacity, rows), 0)
    pick = (slot == every).astype(jnp.bfloat16)
    tile = tile_of(half, 512)
    for c in range(0, width, tile):
        if c % half == 0:
            copies[c // half].wait()
        part = pl.ds(c % half, tile)
        value = jnp.dot(pick, tokens[:, pl.ds(c, tile)], preferred_element_type=jnp.float32)
        value = value.astype(jnp.bfloat16)
        for k in range(experts):
            outs[2 * k + c // half][:, part] = value[k * capacity : (k + 1) * capacity]


def pack(plane, routes, tokens, experts, capacity):
    rows, width = tokens.shape
    outs = pl.pallas_call(
        functools.partial(pack_kernel, experts, capacity),
        out_shape=[jax.ShapeDtypeStruct((capacity, width // 2), jnp.bfloat16)] * (2 * experts),
        in_specs=[SMEM, HBM, HBM],
        out_specs=[VMEM] * (2 * experts),
        scratch_shapes=[
            pltpu.VMEM(routes.shape, routes.dtype),
            pltpu.VMEM(tokens.shape, tokens.dtype),
            pltpu.SemaphoreType.DMA((3,)),
        ],
        cost_estimate=pl.CostEstimate(
            flops=2 * rows * experts * capacity * width,
            bytes_accessed=2 * (rows + experts * capacity) * width,
            transcendentals=0,
        ),
        compiler_params=pltpu.CompilerParams(vmem_limit_bytes=12 << 20),
        name="pack",
    )(plane, held(routes), held(tokens))
    return [tuple(outs[2 * k : 2 * k + 2]) for k in range(experts)]


def place_kernel(experts, capacity, steps, has_base, last, plane_ref, routes_ref, *refs):
    refs = list(refs)
    out = refs.pop()
    scale = turned(refs.pop(0)[...]) if last else None
    base = refs.pop(0) if has_base else None
    row = routes_ref[...]
    rows, width = out.shape
    slot = turned(slots_by_row(row, plane_ref[0], experts, capacity))
    first = lax.broadcasted_iota(jnp.int32, (rows, capacity), 1)
    pick = jnp.concatenate([(slot == first + k * capacity).astype(jnp.float32) for k in steps], axis=1)
    pick = pick.astype(jnp.bfloat16)
    half = width // 2
    tile = tile_of(half, 512)
    for c in range(0, width, tile):
        part, whole = pl.ds(c % half, tile), pl.ds(c, tile)
        data = [refs[2 * n + c // half][:, part] for n in range(len(steps))]
        value = jnp.dot(
            pick, jnp.concatenate(data, axis=0), preferred_element_type=jnp.float32
        )
        if has_base:
            value = value + base[:, whole]
        if last:
            value = scale * value
        out[:, whole] = value.astype(out.dtype)


def place(plane, routes, items, experts, base=None, scale=None):
    rows = routes.shape[1]
    capacity, half = items[0][1][0].shape
    width = 2 * half
    last = scale is not None
    operands = [plane, routes]
    if last:
        operands.append(scale)
    if base is not None:
        operands.append(base)
    for _, halves in items:
        operands += halves
    steps = [k for k, _ in items]
    return pl.pallas_call(
        functools.partial(place_kernel, experts, capacity, steps, base is not None, last),
        out_shape=jax.ShapeDtypeStruct((rows, width), jnp.bfloat16 if last else jnp.float32),
        in_specs=[SMEM] + [VMEM] * (len(operands) - 1),
        out_specs=VMEM,
        cost_estimate=pl.CostEstimate(
            flops=2 * rows * len(items) * capacity * width,
            bytes_accessed=2 * (rows + len(items) * capacity) * width,
            transcendentals=0,
        ),
        compiler_params=pltpu.CompilerParams(vmem_limit_bytes=12 << 20),
        name="place",
    )(*operands)


def stage_kernel(*refs):
    count = (len(refs) - 1) // 2
    sems = refs[-1]
    copies = [
        pltpu.make_async_copy(refs[i], refs[count + i], sems.at[i]) for i in range(count)
    ]
    for copy in copies:
        copy.start()
    for copy in copies:
        copy.wait()


def stage(arrays):
    return pl.pallas_call(
        stage_kernel,
        out_shape=[pltpu.VMEM(a.shape, a.dtype) for a in arrays],
        in_specs=[HBM] * len(arrays),
        out_specs=[VMEM] * len(arrays),
        scratch_shapes=[pltpu.SemaphoreType.DMA((len(arrays),))],
        cost_estimate=pl.CostEstimate(
            flops=0, bytes_accessed=4 * sum(a.size for a in arrays), transcendentals=0
        ),
        compiler_params=pltpu.CompilerParams(vmem_limit_bytes=4 << 20),
        name="stage",
    )(*[held(a) for a in arrays])


def expert_kernel(blocks, hid_tile, *refs):
    ins, refs = refs[: 2 * blocks], refs[2 * blocks :]
    weights, refs = refs[:6], refs[6:]
    outs, refs = refs[: 2 * blocks], refs[2 * blocks :]
    rows, hidden = refs
    capacity, half = ins[0].shape
    hid = hidden.shape[1] // 2
    for i in range(blocks):
        for c in range(2):
            rows[pl.ds(i * capacity, capacity), pl.ds(c * half, half)] = ins[2 * i + c][...]
    x = rows[...]
    for s in range(2):
        gate, up = weights[3 * s], weights[3 * s + 1]
        for h in range(0, hid, hid_tile):
            part = pl.ds(h, hid_tile)
            gate_val = jnp.dot(x, gate[:, part], preferred_element_type=jnp.float32)
            up_val = jnp.dot(x, up[:, part], preferred_element_type=jnp.float32)
            value = gate_val / (1.0 + jnp.exp(-gate_val)) * up_val
            hidden[:, pl.ds(s * hid + h, hid_tile)] = value.astype(jnp.bfloat16)
    tile = tile_of(half, 512)
    for c in range(0, 2 * half, tile):
        part, whole = pl.ds(c % half, tile), pl.ds(c, tile)
        value = jnp.dot(hidden[:, :hid], weights[2][:, whole], preferred_element_type=jnp.float32)
        value += jnp.dot(hidden[:, hid:], weights[5][:, whole], preferred_element_type=jnp.float32)
        value = value.astype(jnp.bfloat16)
        for i in range(blocks):
            outs[2 * i + c // half][:, part] = value[i * capacity : (i + 1) * capacity]


def run_expert(blocks, weights):
    capacity, half = blocks[0][0].shape
    count, total, width = len(blocks), len(blocks) * capacity, 2 * half
    hid = weights[0].shape[1]
    outs = pl.pallas_call(
        functools.partial(expert_kernel, count, tile_of(hid, 256)),
        out_shape=[jax.ShapeDtypeStruct((capacity, half), jnp.bfloat16)] * (2 * count),
        in_specs=[VMEM] * (2 * count + 6),
        out_specs=[VMEM] * (2 * count),
        scratch_shapes=[
            pltpu.VMEM((total, width), jnp.bfloat16),
            pltpu.VMEM((total, 2 * hid), jnp.bfloat16),
        ],
        compiler_params=pltpu.CompilerParams(vmem_limit_bytes=16 << 20),
        cost_estimate=pl.CostEstimate(
            flops=2 * total * width * hid * 6,
            bytes_accessed=12 * width * hid + 4 * total * width,
            transcendentals=total * hid * 2,
        ),
        name="expert",
    )(*[h for block in blocks for h in block], *weights)
    return [tuple(outs[2 * i : 2 * i + 2]) for i in range(count)]


def per_device(tokens, routes, gate_weights, w_gate, w_up, w_down):
    rows = tokens.shape[0]
    experts = lax.axis_size("plane")
    capacity = 2 * rows // experts
    paired = experts & (experts - 1) == 0
    plane = jnp.reshape(lax.axis_index("plane"), (1,)).astype(jnp.int32)
    routes, scale = routes.reshape(1, rows), gate_weights.reshape(1, rows)

    def there(k):
        return [(i, i ^ k if paired else (i + k) % experts) for i in range(experts)]

    def back(k):
        return [(b, a) for a, b in there(k)]

    def both(halves, axis, pairs):
        return tuple(lax.ppermute(x, axis, pairs) for x in halves)

    packed = pack(plane, routes, tokens, experts, capacity)
    own = both(packed[0], "row", SWAP)
    sent = {k: both(packed[k], "plane", there(k)) for k in range(1, experts)}
    weights = [w_gate[0], w_up[0], w_down[0]]
    other = [lax.ppermute(w, "core", SWAP) for w in weights]
    weights = [*stage(weights), *other]

    own_a, own_b = run_expert([packed[0], own], weights)
    items = [(0, own_a), (0, both(own_b, "row", SWAP))]
    for k in range(1, experts):
        met = both(sent[k], "row", SWAP)
        a, b = run_expert([sent[k], met], weights)
        b = both(b, "row", SWAP)
        total = [
            (u.astype(jnp.float32) + v.astype(jnp.float32)).astype(jnp.bfloat16)
            for u, v in zip(a, b)
        ]
        items.append((k, both(total, "plane", back(k))))
    early = [items[0]] + items[3:-1]
    late = [items[1], items[2], items[-1]]
    base = place(plane, routes, early, experts)
    return place(plane, routes, late, experts, base, scale)


def solution(mesh):
    groups, devices = mesh.shape["group"], mesh.shape["expert"]
    experts = devices // SPAN
    fine = Mesh(
        mesh.devices.reshape(groups, experts, SPAN // 2, 2), ("group", "plane", "row", "core")
    )
    every = ("group", "plane", "row", "core")
    expert = ("plane", "row", "core")
    placed = (P(every, None),) * 3 + (P(expert, None, None),) * 3

    return jax.shard_map(
        per_device, mesh=fine, in_specs=placed, out_specs=P(every, None), check_vma=False
    )
```

profile of v0, /device:TPU:0, one launch (start us, length us, event | category | flops | bytes accessed | tf_op | source)
XLA Modules:
  0.0 145.3 jit_solution(14334680695597098369)
XLA Ops:
  0.0 0.5 collective-permute-start.2
  0.5 0.0 collective-permute-start.3
  0.5 0.5 collective-permute-start.4
  1.0 1.9 %pack.1 = (bf16[64,1792]{1,0:T(8,128)(2,1)S(1)}, bf16[64,1792]{1,0:T(8,128)(2,1)S(1)}, bf16[64,1792]{1,0:T(8,128)(2,1)S(1)}, bf16[64,1792]{1,0:T(8,128)(2,1)S(1)...) custom-call(s32[1]{0:T(128)} %bitcast.plane_ref, ...), custom_call_target="tpu_custom_call" | custom-call | flops 234881024 | bytes 2752512 | tf_op jit(solution)/shard_map/pack/pallas_call | solution.py:81
  2.9 4.7 %collective-permute-start.23 = (bf16[64,1792]{1,0:T(8,128)(2,1)S(1)}, bf16[64,1792]{1,0:T(8,128)(2,1)S(1)}, u32[]{:S(2)}, u32[]{:S(2)}) collective-permute-start(bf16[64,1792]{1,0:T(8,128)(2,1)S(1)} %get-tuple-element.53), channel_id=1, source_target_pairs={{0,12},{4,8},{8,4},{12,0},{1,13},{5,9},{9,5},{13,1},{2,14},{6,10},... | collective-permute-start | bytes 688136 | tf_op jit(solution)/shard_map/ppermute | solution.py:251
  7.6 0.1 collective-permute-start.24
  7.6 6.5 %collective-permute-done.23.refs_0_ = bf16[64,1792]{1,0:T(8,128)(2,1)S(1)} collective-permute-done((bf16[64,1792]{1,0:T(8,128)(2,1)S(1)}, bf16[64,1792]{1,0:T(8,128)(2,1)S(1)}, u32[]{:S(2)}, u32[]{:S(2)}) %collective-permute-start.23) | collective-permute-done | bytes 229408 | tf_op jit(solution)/shard_map/ppermute | solution.py:251
  14.1 9.7 %collective-permute-start.15 = (bf16[64,1792]{1,0:T(8,128)(2,1)S(1)}, bf16[64,1792]{1,0:T(8,128)(2,1)S(1)}, u32[]{:S(2)}, u32[]{:S(2)}) collective-permute-start(bf16[64,1792]{1,0:T(8,128)(2,1)S(1)} %get-tuple-element.47), channel_id=1, source_target_pairs={{0,4},{4,0},{8,12},{12,8},{1,5},{5,1},{9,13},{13,9},{2,6},{6,2},{1... | collective-permute-start | bytes 688136 | tf_op jit(solution)/shard_map/ppermute | solution.py:251
  23.9 4.5 %collective-permute-start.16 = (bf16[64,1792]{1,0:T(8,128)(2,1)S(1)}, bf16[64,1792]{1,0:T(8,128)(2,1)S(1)}, u32[]{:S(2)}, u32[]{:S(2)}) collective-permute-start(bf16[64,1792]{1,0:T(8,128)(2,1)S(1)} %get-tuple-element.48), channel_id=1, source_target_pairs={{0,4},{4,0},{8,12},{12,8},{1,5},{5,1},{9,13},{13,9},{2,6},{6,2},{1... | collective-permute-start | bytes 688136 | tf_op jit(solution)/shard_map/ppermute | solution.py:251
  28.3 0.5 collective-permute-done.15.refs_0_
  28.8 1.5 %collective-permute-start.25 = (bf16[64,1792]{1,0:T(8,128)(2,1)S(1)}, bf16[64,1792]{1,0:T(8,128)(2,1)S(1)}, u32[]{:S(2)}, u32[]{:S(2)}) collective-permute-start(bf16[64,1792]{1,0:T(8,128)(2,1)S(1)} %collective-permute-done.23.refs_0_), channel_id=1, source_target_pairs={{0,2},{2,0},{1,3},{3,1},{4,6},{6,4},{5,7},{7,5},{8,10},{10,8},{9,1... | collective-permute-start | bytes 688136 | tf_op jit(solution)/shard_map/ppermute | solution.py:251
  30.3 3.4 %collective-permute-done.16.refs_1_ = bf16[64,1792]{1,0:T(8,128)(2,1)S(1)} collective-permute-done((bf16[64,1792]{1,0:T(8,128)(2,1)S(1)}, bf16[64,1792]{1,0:T(8,128)(2,1)S(1)}, u32[]{:S(2)}, u32[]{:S(2)}) %collective-permute-start.16) | collective-permute-done | bytes 229408 | tf_op jit(solution)/shard_map/ppermute | solution.py:251
  33.7 1.5 %collective-permute-start.26 = (bf16[64,1792]{1,0:T(8,128)(2,1)S(1)}, bf16[64,1792]{1,0:T(8,128)(2,1)S(1)}, u32[]{:S(2)}, u32[]{:S(2)}) collective-permute-start(bf16[64,1792]{1,0:T(8,128)(2,1)S(1)} %collective-permute-done.24.refs_1_), channel_id=1, source_target_pairs={{0,2},{2,0},{1,3},{3,1},{4,6},{6,4},{5,7},{7,5},{8,10},{10,8},{9,1... | collective-permute-start | bytes 688136 | tf_op jit(solution)/shard_map/ppermute | solution.py:251
  35.2 4.2 %stage.1 = (bf16[3584,512]{1,0:T(8,128)(2,1)S(1)}, bf16[3584,512]{1,0:T(8,128)(2,1)S(1)}, bf16[512,3584]{1,0:T(8,128)(2,1)S(1)}) custom-call(bf16[3584,512]{1,0:T(8,128)(2,1)} %bitcast.11, bf16[3584,512]{1,0:T(8,128)(2,1)} %bitcast.13, bf16[512,3584]{1,0:T(8,128)(2,1)} %bitcast.15), custom_call_target="tpu_custom_call" | custom-call | bytes 22020096 | tf_op jit(solution)/shard_map/stage/pallas_call | solution.py:169
  39.5 0.0 collective-permute-done.25.refs_2_
  39.5 2.8 %collective-permute-start.5 = (bf16[64,1792]{1,0:T(8,128)(2,1)S(1)}, bf16[64,1792]{1,0:T(8,128)(2,1)S(1)}, u32[]{:S(2)}, u32[]{:S(2)}) collective-permute-start(bf16[64,1792]{1,0:T(8,128)(2,1)S(1)} %get-tuple-element.39), channel_id=1, source_target_pairs={{0,8},{4,12},{8,0},{12,4},{1,9},{5,13},{9,1},{13,5},{2,10},{6,14},... | collective-permute-start | bytes 688136 | tf_op jit(solution)/shard_map/ppermute | solution.py:251
  42.3 0.5 collective-permute-start.6
  42.8 0.0 collective-permute-done.2.refs_7_
  42.8 1.5 %collective-permute-start = (bf16[64,1792]{1,0:T(8,128)(2,1)S(1)}, bf16[64,1792]{1,0:T(8,128)(2,1)S(1)}, u32[]{:S(2)}, u32[]{:S(2)}) collective-permute-start(bf16[64,1792]{1,0:T(8,128)(2,1)S(1)} %get-tuple-element.32.refs_0_), channel_id=1, source_target_pairs={{0,2},{2,0},{1,3},{3,1},{4,6},{6,4},{5,7},{7,5},{8,10},{10,8},{9,1... | collective-permute-start | bytes 688136 | tf_op jit(solution)/shard_map/ppermute | solution.py:251
  44.3 0.5 collective-permute-start.17
  44.8 0.0 collective-permute-done.4.refs_9_
  44.8 1.5 %collective-permute-start.18 = (bf16[64,1792]{1,0:T(8,128)(2,1)S(1)}, bf16[64,1792]{1,0:T(8,128)(2,1)S(1)}, u32[]{:S(2)}, u32[]{:S(2)}) collective-permute-start(bf16[64,1792]{1,0:T(8,128)(2,1)S(1)} %collective-permute-done.16.refs_1_), channel_id=1, source_target_pairs={{0,2},{2,0},{1,3},{3,1},{4,6},{6,4},{5,7},{7,5},{8,10},{10,8},{9,1... | collective-permute-start | bytes 688136 | tf_op jit(solution)/shard_map/ppermute | solution.py:251
  46.4 7.3 %expert.7 = (bf16[64,1792]{1,0:T(8,128)(2,1)S(1)}, bf16[64,1792]{1,0:T(8,128)(2,1)S(1)}, bf16[64,1792]{1,0:T(8,128)(2,1)S(1)}, bf16[64,1792]{1,0:T(8,128)(2,1)S(1)}) custom-call(bf16[64,1792]{1,0:T(8,128)(2,1)S(1)} %collective-permute-done.23.refs_0_, bf16[64,1792]{1,0:T(8,128)(2,1)S(1)} %collective-permute-done.24.refs_1_, ...), custom_call_target="tpu_custom_call" | custom-call | flops 2818572288 | bytes 23855104 | tf_op jit(solution)/shard_map/expert/pallas_call | solution.py:216
  53.7 3.9 %collective-permute-done.5.refs_0_ = bf16[64,1792]{1,0:T(8,128)(2,1)S(1)} collective-permute-done((bf16[64,1792]{1,0:T(8,128)(2,1)S(1)}, bf16[64,1792]{1,0:T(8,128)(2,1)S(1)}, u32[]{:S(2)}, u32[]{:S(2)}) %collective-permute-start.5) | collective-permute-done | bytes 229408 | tf_op jit(solution)/shard_map/ppermute | solution.py:251
  57.6 0.5 collective-permute-start.1
  58.1 3.4 %collective-permute-done.6.refs_1_ = bf16[64,1792]{1,0:T(8,128)(2,1)S(1)} collective-permute-done((bf16[64,1792]{1,0:T(8,128)(2,1)S(1)}, bf16[64,1792]{1,0:T(8,128)(2,1)S(1)}, u32[]{:S(2)}, u32[]{:S(2)}) %collective-permute-start.6) | collective-permute-done | bytes 229408 | tf_op jit(solution)/shard_map/ppermute | solution.py:251
  61.5 0.5 collective-permute-start.7
  62.0 0.0 collective-permute-done.17.refs_2_
  62.0 1.5 %collective-permute-start.8 = (bf16[64,1792]{1,0:T(8,128)(2,1)S(1)}, bf16[64,1792]{1,0:T(8,128)(2,1)S(1)}, u32[]{:S(2)}, u32[]{:S(2)}) collective-permute-start(bf16[64,1792]{1,0:T(8,128)(2,1)S(1)} %collective-permute-done.6.refs_1_), channel_id=1, source_target_pairs={{0,2},{2,0},{1,3},{3,1},{4,6},{6,4},{5,7},{7,5},{8,10},{10,8},{9,1... | collective-permute-start | bytes 688136 | tf_op jit(solution)/shard_map/ppermute | solution.py:251
  63.5 0.5 collective-permute-start.29
  64.1 7.3 %expert.6 = (bf16[64,1792]{1,0:T(8,128)(2,1)S(1)}, bf16[64,1792]{1,0:T(8,128)(2,1)S(1)}, bf16[64,1792]{1,0:T(8,128)(2,1)S(1)}, bf16[64,1792]{1,0:T(8,128)(2,1)S(1)}) custom-call(bf16[64,1792]{1,0:T(8,128)(2,1)S(1)} %collective-permute-done.15.refs_0_, bf16[64,1792]{1,0:T(8,128)(2,1)S(1)} %collective-permute-done.16.refs_1_, ...), custom_call_target="tpu_custom_call" | custom-call | flops 2818572288 | bytes 23855104 | tf_op jit(solution)/shard_map/expert/pallas_call | solution.py:216
  71.4 0.0 collective-permute-done.7.refs_2_
  71.4 1.6 %collective-permute-start.27 = (bf16[64,1792]{1,0:T(8,128)(2,1)S(1)}, bf16[64,1792]{1,0:T(8,128)(2,1)S(1)}, u32[]{:S(2)}, u32[]{:S(2)}) collective-permute-start(bf16[64,1792]{1,0:T(8,128)(2,1)S(1)} %get-tuple-element.56), channel_id=1, source_target_pairs={{0,2},{2,0},{1,3},{3,1},{4,6},{6,4},{5,7},{7,5},{8,10},{10,8},{9,1... | collective-permute-start | bytes 688136 | tf_op jit(solution)/shard_map/ppermute | solution.py:251
  73.0 1.9 %collective-permute-done.8.refs_3_ = bf16[64,1792]{1,0:T(8,128)(2,1)S(1)} collective-permute-done((bf16[64,1792]{1,0:T(8,128)(2,1)S(1)}, bf16[64,1792]{1,0:T(8,128)(2,1)S(1)}, u32[]{:S(2)}, u32[]{:S(2)}) %collective-permute-start.8) | collective-permute-done | bytes 229408 | tf_op jit(solution)/shard_map/ppermute | solution.py:251
  74.9 0.5 collective-permute-start.21
  75.4 7.3 %expert.5 = (bf16[64,1792]{1,0:T(8,128)(2,1)S(1)}, bf16[64,1792]{1,0:T(8,128)(2,1)S(1)}, bf16[64,1792]{1,0:T(8,128)(2,1)S(1)}, bf16[64,1792]{1,0:T(8,128)(2,1)S(1)}) custom-call(bf16[64,1792]{1,0:T(8,128)(2,1)S(1)} %collective-permute-done.5.refs_0_, bf16[64,1792]{1,0:T(8,128)(2,1)S(1)} %collective-permute-done.6.refs_1_, ...), custom_call_target="tpu_custom_call" | custom-call | flops 2818572288 | bytes 23855104 | tf_op jit(solution)/shard_map/expert/pallas_call | solution.py:216
  82.8 1.6 %collective-permute-start.19 = (bf16[64,1792]{1,0:T(8,128)(2,1)S(1)}, bf16[64,1792]{1,0:T(8,128)(2,1)S(1)}, u32[]{:S(2)}, u32[]{:S(2)}) collective-permute-start(bf16[64,1792]{1,0:T(8,128)(2,1)S(1)} %get-tuple-element.50), channel_id=1, source_target_pairs={{0,2},{2,0},{1,3},{3,1},{4,6},{6,4},{5,7},{7,5},{8,10},{10,8},{9,1... | collective-permute-start | bytes 688136 | tf_op jit(solution)/shard_map/ppermute | solution.py:251
  84.3 0.0 collective-permute-done.1.refs_3_
  84.3 0.5 collective-permute-start.11
  84.9 7.5 %expert.4 = (bf16[64,1792]{1,0:T(8,128)(2,1)S(1)}, bf16[64,1792]{1,0:T(8,128)(2,1)S(1)}, bf16[64,1792]{1,0:T(8,128)(2,1)S(1)}, bf16[64,1792]{1,0:T(8,128)(2,1)S(1)}) custom-call(bf16[64,1792]{1,0:T(8,128)(2,1)S(1)} %get-tuple-element.32.refs_0_, bf16[64,1792]{1,0:T(8,128)(2,1)S(1)} %get-tuple-element.33.refs_1_, ...), custom_call_target="tpu_custom_call" | custom-call | flops 2818572288 | bytes 23855104 | tf_op jit(solution)/shard_map/expert/pallas_call | solution.py:216
  92.4 0.0 copy-start
  92.4 0.0 copy-start.1
  92.4 1.6 %collective-permute-start.9 = (bf16[64,1792]{1,0:T(8,128)(2,1)S(1)}, bf16[64,1792]{1,0:T(8,128)(2,1)S(1)}, u32[]{:S(2)}, u32[]{:S(2)}) collective-permute-start(bf16[64,1792]{1,0:T(8,128)(2,1)S(1)} %get-tuple-element.42), channel_id=1, source_target_pairs={{0,2},{2,0},{1,3},{3,1},{4,6},{6,4},{5,7},{7,5},{8,10},{10,8},{9,1... | collective-permute-start | bytes 688136 | tf_op jit(solution)/shard_map/ppermute | solution.py:251
  94.0 0.1 add_convert_fusion
  94.1 0.6 collective-permute-start.13
  94.7 0.1 add_convert_fusion.1
  94.7 1.6 %collective-permute-start.14 = (bf16[64,1792]{1,0:T(8,128)(2,1)S(1)}, bf16[64,1792]{1,0:T(8,128)(2,1)S(1)}, u32[]{:S(2)}, u32[]{:S(2)}) collective-permute-start(bf16[64,1792]{1,0:T(8,128)(2,1)S(1)} %get-tuple-element.46), channel_id=1, source_target_pairs={{0,2},{2,0},{1,3},{3,1},{4,6},{6,4},{5,7},{7,5},{8,10},{10,8},{9,1... | collective-permute-start | bytes 688136 | tf_op jit(solution)/shard_map/ppermute | solution.py:251
  96.3 0.1 add_convert_fusion.2
  96.4 3.1 %collective-permute-done.11 = bf16[64,1792]{1,0:T(8,128)(2,1)S(1)} collective-permute-done((bf16[64,1792]{1,0:T(8,128)(2,1)S(1)}, bf16[64,1792]{1,0:T(8,128)(2,1)S(1)}, u32[]{:S(2)}, u32[]{:S(2)}) %collective-permute-start.11) | collective-permute-done | bytes 229408 | tf_op jit(solution)/shard_map/ppermute | solution.py:251
  99.5 2.5 %collective-permute-start.30 = (bf16[64,1792]{1,0:T(8,128)(2,1)S(1)}, bf16[64,1792]{1,0:T(8,128)(2,1)S(1)}, u32[]{:S(2)}, u32[]{:S(2)}) collective-permute-start(bf16[64,1792]{1,0:T(8,128)(2,1)S(1)} %add_convert_fusion), channel_id=1, source_target_pairs={{12,0},{8,4},{4,8},{0,12},{13,1},{9,5},{5,9},{1,13},{14,2},{10,6},... | collective-permute-start | bytes 688136 | tf_op jit(solution)/shard_map/ppermute | solution.py:251
  102.0 0.1 add_convert_fusion.4
  102.0 2.4 %collective-permute-done.9 = bf16[64,1792]{1,0:T(8,128)(2,1)S(1)} collective-permute-done((bf16[64,1792]{1,0:T(8,128)(2,1)S(1)}, bf16[64,1792]{1,0:T(8,128)(2,1)S(1)}, u32[]{:S(2)}, u32[]{:S(2)}) %collective-permute-start.9) | collective-permute-done | bytes 229408 | tf_op jit(solution)/shard_map/ppermute | solution.py:251
  104.4 3.1 %collective-permute-start.12 = (bf16[64,1792]{1,0:T(8,128)(2,1)S(1)}, bf16[64,1792]{1,0:T(8,128)(2,1)S(1)}, u32[]{:S(2)}, u32[]{:S(2)}) collective-permute-start(bf16[64,1792]{1,0:T(8,128)(2,1)S(1)} %add_convert_fusion.4), channel_id=1, source_target_pairs={{8,0},{12,4},{0,8},{4,12},{9,1},{13,5},{1,9},{5,13},{10,2},{14,6},... | collective-permute-start | bytes 688136 | tf_op jit(solution)/shard_map/ppermute | solution.py:251
  107.5 0.1 add_convert_fusion.5
  107.6 0.1 collective-permute-start.10
  107.6 0.1 add_convert_fusion.3
  107.7 1.6 %collective-permute-done.13.refs_2_ = bf16[64,1792]{1,0:T(8,128)(2,1)S(1)} collective-permute-done((bf16[64,1792]{1,0:T(8,128)(2,1)S(1)}, bf16[64,1792]{1,0:T(8,128)(2,1)S(1)}, u32[]{:S(2)}, u32[]{:S(2)}) %collective-permute-start.13) | collective-permute-done | bytes 229408 | tf_op jit(solution)/shard_map/ppermute | solution.py:251
  109.3 2.5 %collective-permute-start.28 = (bf16[64,1792]{1,0:T(8,128)(2,1)S(1)}, bf16[64,1792]{1,0:T(8,128)(2,1)S(1)}, u32[]{:S(2)}, u32[]{:S(2)}) collective-permute-start(bf16[64,1792]{1,0:T(8,128)(2,1)S(1)} %add_convert_fusion.1), channel_id=1, source_target_pairs={{12,0},{8,4},{4,8},{0,12},{13,1},{9,5},{5,9},{1,13},{14,2},{10,6},... | collective-permute-start | bytes 688136 | tf_op jit(solution)/shard_map/ppermute | solution.py:251
  111.8 19.1 %collective-permute-done.12.refs_3_ = bf16[64,1792]{1,0:T(8,128)(2,1)S(1)} collective-permute-done((bf16[64,1792]{1,0:T(8,128)(2,1)S(1)}, bf16[64,1792]{1,0:T(8,128)(2,1)S(1)}, u32[]{:S(2)}, u32[]{:S(2)}) %collective-permute-start.12) | collective-permute-done | bytes 229408 | tf_op jit(solution)/shard_map/ppermute | solution.py:251
  130.9 4.9 %collective-permute-done.10.refs_2_ = bf16[64,1792]{1,0:T(8,128)(2,1)S(1)} collective-permute-done((bf16[64,1792]{1,0:T(8,128)(2,1)S(1)}, bf16[64,1792]{1,0:T(8,128)(2,1)S(1)}, u32[]{:S(2)}, u32[]{:S(2)}) %collective-permute-start.10) | collective-permute-done | bytes 229408 | tf_op jit(solution)/shard_map/ppermute | solution.py:251
  135.8 0.6 place.2.refs_1_
  136.4 3.6 %collective-permute-done.22.refs_5_ = bf16[64,1792]{1,0:T(8,128)(2,1)S(1)} collective-permute-done((bf16[64,1792]{1,0:T(8,128)(2,1)S(1)}, bf16[64,1792]{1,0:T(8,128)(2,1)S(1)}, u32[]{:S(2)}, u32[]{:S(2)}) %collective-permute-start.22) | collective-permute-done | bytes 229408 | tf_op jit(solution)/shard_map/ppermute | solution.py:251
  140.0 3.7 %collective-permute-done.20.refs_4_ = bf16[64,1792]{1,0:T(8,128)(2,1)S(1)} collective-permute-done((bf16[64,1792]{1,0:T(8,128)(2,1)S(1)}, bf16[64,1792]{1,0:T(8,128)(2,1)S(1)}, u32[]{:S(2)}, u32[]{:S(2)}) %collective-permute-start.20) | collective-permute-done | bytes 229408 | tf_op jit(solution)/shard_map/ppermute | solution.py:251
  143.7 1.6 %place.3 = bf16[128,3584]{1,0:T(8,128)(2,1)} custom-call(s32[1]{0:T(128)} %bitcast.plane_ref, s32[1,128]{1,0:T(1,128)S(1)} %bitcast.8, f32[1,128]{1,0:T(1,128)S(1)} %bitcast.9, f32[128,3584]{1,0:T(8,128)S(1)} %place.2.refs_1_, bf16[64,1792]{1,0:T(8,128)(2,1)S(1)} %collective-permute-done.13.refs_2_, bf16[64,1792]{1,0:T(8,128)(2,1)S(1)} %collective-permute-done.14.refs_3_, ...), custom_call_target="tpu_custom_call" | custom-call | flops 176160768 | bytes 2293760 | tf_op jit(solution)/shard_map/place/pallas_call | solution.py:141
  (16 shorter events, 0.0 us)
Async XLA Ops:
  0.0 42.8 %collective-permute-start.2 = (bf16[3584,512]{1,0:T(8,128)(2,1)}, bf16[3584,512]{1,0:T(8,128)(2,1)}, u32[]{:S(2)}, u32[]{:S(2)}) collective-permute-start(bf16[3584,512]{1,0:T(8,128)(2,1)} %bitcast.10), channel_id=1, source_target_pairs={{0,1},{1,0},{2,3},{3,2},{4,5},{5,4},{6,7},{7,6},{8,9},{9,8},{10,11... | collective-permute-start | bytes 11010056 | tf_op jit(solution)/shard_map/ppermute | solution.py:257
  0.5 43.8 %collective-permute-start.3 = (bf16[3584,512]{1,0:T(8,128)(2,1)}, bf16[3584,512]{1,0:T(8,128)(2,1)}, u32[]{:S(2)}, u32[]{:S(2)}) collective-permute-start(bf16[3584,512]{1,0:T(8,128)(2,1)} %bitcast.12), channel_id=1, source_target_pairs={{0,1},{1,0},{2,3},{3,2},{4,5},{5,4},{6,7},{7,6},{8,9},{9,8},{10,11... | collective-permute-start | bytes 11010056 | tf_op jit(solution)/shard_map/ppermute | solution.py:257
  0.5 44.3 %collective-permute-start.4 = (bf16[512,3584]{1,0:T(8,128)(2,1)}, bf16[512,3584]{1,0:T(8,128)(2,1)}, u32[]{:S(2)}, u32[]{:S(2)}) collective-permute-start(bf16[512,3584]{1,0:T(8,128)(2,1)} %bitcast.14), channel_id=1, source_target_pairs={{0,1},{1,0},{2,3},{3,2},{4,5},{5,4},{6,7},{7,6},{8,9},{9,8},{10,11... | collective-permute-start | bytes 11010056 | tf_op jit(solution)/shard_map/ppermute | solution.py:257
  2.9 11.2 %collective-permute-start.23 = (bf16[64,1792]{1,0:T(8,128)(2,1)S(1)}, bf16[64,1792]{1,0:T(8,128)(2,1)S(1)}, u32[]{:S(2)}, u32[]{:S(2)}) collective-permute-start(bf16[64,1792]{1,0:T(8,128)(2,1)S(1)} %get-tuple-element.53), channel_id=1, source_target_pairs={{0,12},{4,8},{8,4},{12,0},{1,13},{5,9},{9,5},{13,1},{2,14},{6,10},... | collective-permute-start | bytes 688136 | tf_op jit(solution)/shard_map/ppermute | solution.py:251
  7.6 16.3 %collective-permute-start.24 = (bf16[64,1792]{1,0:T(8,128)(2,1)S(1)}, bf16[64,1792]{1,0:T(8,128)(2,1)S(1)}, u32[]{:S(2)}, u32[]{:S(2)}) collective-permute-start(bf16[64,1792]{1,0:T(8,128)(2,1)S(1)} %get-tuple-element.54), channel_id=1, source_target_pairs={{0,12},{4,8},{8,4},{12,0},{1,13},{5,9},{9,5},{13,1},{2,14},{6,10},... | collective-permute-start | bytes 688136 | tf_op jit(solution)/shard_map/ppermute | solution.py:251
  14.1 14.7 %collective-permute-start.15 = (bf16[64,1792]{1,0:T(8,128)(2,1)S(1)}, bf16[64,1792]{1,0:T(8,128)(2,1)S(1)}, u32[]{:S(2)}, u32[]{:S(2)}) collective-permute-start(bf16[64,1792]{1,0:T(8,128)(2,1)S(1)} %get-tuple-element.47), channel_id=1, source_target_pairs={{0,4},{4,0},{8,12},{12,8},{1,5},{5,1},{9,13},{13,9},{2,6},{6,2},{1... | collective-permute-start | bytes 688136 | tf_op jit(solution)/shard_map/ppermute | solution.py:251
  23.9 9.9 %collective-permute-start.16 = (bf16[64,1792]{1,0:T(8,128)(2,1)S(1)}, bf16[64,1792]{1,0:T(8,128)(2,1)S(1)}, u32[]{:S(2)}, u32[]{:S(2)}) collective-permute-start(bf16[64,1792]{1,0:T(8,128)(2,1)S(1)} %get-tuple-element.48), channel_id=1, source_target_pairs={{0,4},{4,0},{8,12},{12,8},{1,5},{5,1},{9,13},{13,9},{2,6},{6,2},{1... | collective-permute-start | bytes 688136 | tf_op jit(solution)/shard_map/ppermute | solution.py:251
  28.8 10.7 %collective-permute-start.25 = (bf16[64,1792]{1,0:T(8,128)(2,1)S(1)}, bf16[64,1792]{1,0:T(8,128)(2,1)S(1)}, u32[]{:S(2)}, u32[]{:S(2)}) collective-permute-start(bf16[64,1792]{1,0:T(8,128)(2,1)S(1)} %collective-permute-done.23.refs_0_), channel_id=1, source_target_pairs={{0,2},{2,0},{1,3},{3,1},{4,6},{6,4},{5,7},{7,5},{8,10},{10,8},{9,1... | collective-permute-start | bytes 688136 | tf_op jit(solution)/shard_map/ppermute | solution.py:251
  33.7 8.6 %collective-permute-start.26 = (bf16[64,1792]{1,0:T(8,128)(2,1)S(1)}, bf16[64,1792]{1,0:T(8,128)(2,1)S(1)}, u32[]{:S(2)}, u32[]{:S(2)}) collective-permute-start(bf16[64,1792]{1,0:T(8,128)(2,1)S(1)} %collective-permute-done.24.refs_1_), channel_id=1, source_target_pairs={{0,2},{2,0},{1,3},{3,1},{4,6},{6,4},{5,7},{7,5},{8,10},{10,8},{9,1... | collective-permute-start | bytes 688136 | tf_op jit(solution)/shard_map/ppermute | solution.py:251
  39.5 18.1 %collective-permute-start.5 = (bf16[64,1792]{1,0:T(8,128)(2,1)S(1)}, bf16[64,1792]{1,0:T(8,128)(2,1)S(1)}, u32[]{:S(2)}, u32[]{:S(2)}) collective-permute-start(bf16[64,1792]{1,0:T(8,128)(2,1)S(1)} %get-tuple-element.39), channel_id=1, source_target_pairs={{0,8},{4,12},{8,0},{12,4},{1,9},{5,13},{9,1},{13,5},{2,10},{6,14},... | collective-permute-start | bytes 688136 | tf_op jit(solution)/shard_map/ppermute | solution.py:251
  42.3 19.2 %collective-permute-start.6 = (bf16[64,1792]{1,0:T(8,128)(2,1)S(1)}, bf16[64,1792]{1,0:T(8,128)(2,1)S(1)}, u32[]{:S(2)}, u32[]{:S(2)}) collective-permute-start(bf16[64,1792]{1,0:T(8,128)(2,1)S(1)} %get-tuple-element.40), channel_id=1, source_target_pairs={{0,8},{4,12},{8,0},{12,4},{1,9},{5,13},{9,1},{13,5},{2,10},{6,14},... | collective-permute-start | bytes 688136 | tf_op jit(solution)/shard_map/ppermute | solution.py:251
  42.8 40.0 %collective-permute-start = (bf16[64,1792]{1,0:T(8,128)(2,1)S(1)}, bf16[64,1792]{1,0:T(8,128)(2,1)S(1)}, u32[]{:S(2)}, u32[]{:S(2)}) collective-permute-start(bf16[64,1792]{1,0:T(8,128)(2,1)S(1)} %get-tuple-element.32.refs_0_), channel_id=1, source_target_pairs={{0,2},{2,0},{1,3},{3,1},{4,6},{6,4},{5,7},{7,5},{8,10},{10,8},{9,1... | collective-permute-start | bytes 688136 | tf_op jit(solution)/shard_map/ppermute | solution.py:251
  44.3 17.7 %collective-permute-start.17 = (bf16[64,1792]{1,0:T(8,128)(2,1)S(1)}, bf16[64,1792]{1,0:T(8,128)(2,1)S(1)}, u32[]{:S(2)}, u32[]{:S(2)}) collective-permute-start(bf16[64,1792]{1,0:T(8,128)(2,1)S(1)} %collective-permute-done.15.refs_0_), channel_id=1, source_target_pairs={{0,2},{2,0},{1,3},{3,1},{4,6},{6,4},{5,7},{7,5},{8,10},{10,8},{9,1... | collective-permute-start | bytes 688136 | tf_op jit(solution)/shard_map/ppermute | solution.py:251
  44.8 18.7 %collective-permute-start.18 = (bf16[64,1792]{1,0:T(8,128)(2,1)S(1)}, bf16[64,1792]{1,0:T(8,128)(2,1)S(1)}, u32[]{:S(2)}, u32[]{:S(2)}) collective-permute-start(bf16[64,1792]{1,0:T(8,128)(2,1)S(1)} %collective-permute-done.16.refs_1_), channel_id=1, source_target_pairs={{0,2},{2,0},{1,3},{3,1},{4,6},{6,4},{5,7},{7,5},{8,10},{10,8},{9,1... | collective-permute-start | bytes 688136 | tf_op jit(solution)/shard_map/ppermute | solution.py:251
  57.6 26.8 %collective-permute-start.1 = (bf16[64,1792]{1,0:T(8,128)(2,1)S(1)}, bf16[64,1792]{1,0:T(8,128)(2,1)S(1)}, u32[]{:S(2)}, u32[]{:S(2)}) collective-permute-start(bf16[64,1792]{1,0:T(8,128)(2,1)S(1)} %get-tuple-element.33.refs_1_), channel_id=1, source_target_pairs={{0,2},{2,0},{1,3},{3,1},{4,6},{6,4},{5,7},{7,5},{8,10},{10,8},{9,1... | collective-permute-start | bytes 688136 | tf_op jit(solution)/shard_map/ppermute | solution.py:251
  61.5 9.9 %collective-permute-start.7 = (bf16[64,1792]{1,0:T(8,128)(2,1)S(1)}, bf16[64,1792]{1,0:T(8,128)(2,1)S(1)}, u32[]{:S(2)}, u32[]{:S(2)}) collective-permute-start(bf16[64,1792]{1,0:T(8,128)(2,1)S(1)} %collective-permute-done.5.refs_0_), channel_id=1, source_target_pairs={{0,2},{2,0},{1,3},{3,1},{4,6},{6,4},{5,7},{7,5},{8,10},{10,8},{9,1... | collective-permute-start | bytes 688136 | tf_op jit(solution)/shard_map/ppermute | solution.py:251
  62.0 12.9 %collective-permute-start.8 = (bf16[64,1792]{1,0:T(8,128)(2,1)S(1)}, bf16[64,1792]{1,0:T(8,128)(2,1)S(1)}, u32[]{:S(2)}, u32[]{:S(2)}) collective-permute-start(bf16[64,1792]{1,0:T(8,128)(2,1)S(1)} %collective-permute-done.6.refs_1_), channel_id=1, source_target_pairs={{0,2},{2,0},{1,3},{3,1},{4,6},{6,4},{5,7},{7,5},{8,10},{10,8},{9,1... | collective-permute-start | bytes 688136 | tf_op jit(solution)/shard_map/ppermute | solution.py:251
  63.5 28.9 %collective-permute-start.29 = (bf16[64,1792]{1,0:T(8,128)(2,1)S(1)}, bf16[64,1792]{1,0:T(8,128)(2,1)S(1)}, u32[]{:S(2)}, u32[]{:S(2)}) collective-permute-start(bf16[64,1792]{1,0:T(8,128)(2,1)S(1)} %get-tuple-element.58), channel_id=1, source_target_pairs={{0,2},{2,0},{1,3},{3,1},{4,6},{6,4},{5,7},{7,5},{8,10},{10,8},{9,1... | collective-permute-start | bytes 688136 | tf_op jit(solution)/shard_map/ppermute | solution.py:251
  71.4 22.7 %collective-permute-start.27 = (bf16[64,1792]{1,0:T(8,128)(2,1)S(1)}, bf16[64,1792]{1,0:T(8,128)(2,1)S(1)}, u32[]{:S(2)}, u32[]{:S(2)}) collective-permute-start(bf16[64,1792]{1,0:T(8,128)(2,1)S(1)} %get-tuple-element.56), channel_id=1, source_target_pairs={{0,2},{2,0},{1,3},{3,1},{4,6},{6,4},{5,7},{7,5},{8,10},{10,8},{9,1... | collective-permute-start | bytes 688136 | tf_op jit(solution)/shard_map/ppermute | solution.py:251
  74.9 19.8 %collective-permute-start.21 = (bf16[64,1792]{1,0:T(8,128)(2,1)S(1)}, bf16[64,1792]{1,0:T(8,128)(2,1)S(1)}, u32[]{:S(2)}, u32[]{:S(2)}) collective-permute-start(bf16[64,1792]{1,0:T(8,128)(2,1)S(1)} %get-tuple-element.52), channel_id=1, source_target_pairs={{0,2},{2,0},{1,3},{3,1},{4,6},{6,4},{5,7},{7,5},{8,10},{10,8},{9,1... | collective-permute-start | bytes 688136 | tf_op jit(solution)/shard_map/ppermute | solution.py:251
  82.8 24.8 %collective-permute-start.19 = (bf16[64,1792]{1,0:T(8,128)(2,1)S(1)}, bf16[64,1792]{1,0:T(8,128)(2,1)S(1)}, u32[]{:S(2)}, u32[]{:S(2)}) collective-permute-start(bf16[64,1792]{1,0:T(8,128)(2,1)S(1)} %get-tuple-element.50), channel_id=1, source_target_pairs={{0,2},{2,0},{1,3},{3,1},{4,6},{6,4},{5,7},{7,5},{8,10},{10,8},{9,1... | collective-permute-start | bytes 688136 | tf_op jit(solution)/shard_map/ppermute | solution.py:251
  84.3 15.1 %collective-permute-start.11 = (bf16[64,1792]{1,0:T(8,128)(2,1)S(1)}, bf16[64,1792]{1,0:T(8,128)(2,1)S(1)}, u32[]{:S(2)}, u32[]{:S(2)}) collective-permute-start(bf16[64,1792]{1,0:T(8,128)(2,1)S(1)} %get-tuple-element.44), channel_id=1, source_target_pairs={{0,2},{2,0},{1,3},{3,1},{4,6},{6,4},{5,7},{7,5},{8,10},{10,8},{9,1... | collective-permute-start | bytes 688136 | tf_op jit(solution)/shard_map/ppermute | solution.py:251
  92.4 43.4 %copy-start = (s32[128,1]{0,1:T(1,128)S(1)}, s32[128,1]{0,1:T(1,128)}, u32[]{:S(2)}) copy-start(s32[128,1]{0,1:T(1,128)} %param.7) | copy-start | bytes 1540
  92.4 51.3 %copy-start.1 = (f32[128,1]{0,1:T(1,128)S(1)}, f32[128,1]{0,1:T(1,128)}, u32[]{:S(2)}) copy-start(f32[128,1]{0,1:T(1,128)} %param.8) | copy-start | bytes 1540
  92.4 12.0 %collective-permute-start.9 = (bf16[64,1792]{1,0:T(8,128)(2,1)S(1)}, bf16[64,1792]{1,0:T(8,128)(2,1)S(1)}, u32[]{:S(2)}, u32[]{:S(2)}) collective-permute-start(bf16[64,1792]{1,0:T(8,128)(2,1)S(1)} %get-tuple-element.42), channel_id=1, source_target_pairs={{0,2},{2,0},{1,3},{3,1},{4,6},{6,4},{5,7},{7,5},{8,10},{10,8},{9,1... | collective-permute-start | bytes 688136 | tf_op jit(solution)/shard_map/ppermute | solution.py:251
  94.1 15.2 %collective-permute-start.13 = (bf16[64,1792]{1,0:T(8,128)(2,1)S(1)}, bf16[64,1792]{1,0:T(8,128)(2,1)S(1)}, u32[]{:S(2)}, u32[]{:S(2)}) collective-permute-start(bf16[64,1792]{1,0:T(8,128)(2,1)S(1)} %get-tuple-element.45), channel_id=1, source_target_pairs={{0,2},{2,0},{1,3},{3,1},{4,6},{6,4},{5,7},{7,5},{8,10},{10,8},{9,1... | collective-permute-start | bytes 688136 | tf_op jit(solution)/shard_map/ppermute | solution.py:251
  94.7 41.7 %collective-permute-start.14 = (bf16[64,1792]{1,0:T(8,128)(2,1)S(1)}, bf16[64,1792]{1,0:T(8,128)(2,1)S(1)}, u32[]{:S(2)}, u32[]{:S(2)}) collective-permute-start(bf16[64,1792]{1,0:T(8,128)(2,1)S(1)} %get-tuple-element.46), channel_id=1, source_target_pairs={{0,2},{2,0},{1,3},{3,1},{4,6},{6,4},{5,7},{7,5},{8,10},{10,8},{9,1... | collective-permute-start | bytes 688136 | tf_op jit(solution)/shard_map/ppermute | solution.py:251
  99.5 37.0 %collective-permute-start.30 = (bf16[64,1792]{1,0:T(8,128)(2,1)S(1)}, bf16[64,1792]{1,0:T(8,128)(2,1)S(1)}, u32[]{:S(2)}, u32[]{:S(2)}) collective-permute-start(bf16[64,1792]{1,0:T(8,128)(2,1)S(1)} %add_convert_fusion), channel_id=1, source_target_pairs={{12,0},{8,4},{4,8},{0,12},{13,1},{9,5},{5,9},{1,13},{14,2},{10,6},... | collective-permute-start | bytes 688136 | tf_op jit(solution)/shard_map/ppermute | solution.py:251
  104.4 26.5 %collective-permute-start.12 = (bf16[64,1792]{1,0:T(8,128)(2,1)S(1)}, bf16[64,1792]{1,0:T(8,128)(2,1)S(1)}, u32[]{:S(2)}, u32[]{:S(2)}) collective-permute-start(bf16[64,1792]{1,0:T(8,128)(2,1)S(1)} %add_convert_fusion.4), channel_id=1, source_target_pairs={{8,0},{12,4},{0,8},{4,12},{9,1},{13,5},{1,9},{5,13},{10,2},{14,6},... | collective-permute-start | bytes 688136 | tf_op jit(solution)/shard_map/ppermute | solution.py:251
  107.6 28.2 %collective-permute-start.10 = (bf16[64,1792]{1,0:T(8,128)(2,1)S(1)}, bf16[64,1792]{1,0:T(8,128)(2,1)S(1)}, u32[]{:S(2)}, u32[]{:S(2)}) collective-permute-start(bf16[64,1792]{1,0:T(8,128)(2,1)S(1)} %add_convert_fusion.5), channel_id=1, source_target_pairs={{8,0},{12,4},{0,8},{4,12},{9,1},{13,5},{1,9},{5,13},{10,2},{14,6},... | collective-permute-start | bytes 688136 | tf_op jit(solution)/shard_map/ppermute | solution.py:251
  109.3 27.1 %collective-permute-start.28 = (bf16[64,1792]{1,0:T(8,128)(2,1)S(1)}, bf16[64,1792]{1,0:T(8,128)(2,1)S(1)}, u32[]{:S(2)}, u32[]{:S(2)}) collective-permute-start(bf16[64,1792]{1,0:T(8,128)(2,1)S(1)} %add_convert_fusion.1), channel_id=1, source_target_pairs={{12,0},{8,4},{4,8},{0,12},{13,1},{9,5},{5,9},{1,13},{14,2},{10,6},... | collective-permute-start | bytes 688136 | tf_op jit(solution)/shard_map/ppermute | solution.py:251
  130.9 9.1 %collective-permute-start.22 = (bf16[64,1792]{1,0:T(8,128)(2,1)S(1)}, bf16[64,1792]{1,0:T(8,128)(2,1)S(1)}, u32[]{:S(2)}, u32[]{:S(2)}) collective-permute-start(bf16[64,1792]{1,0:T(8,128)(2,1)S(1)} %add_convert_fusion.2), channel_id=1, source_target_pairs={{4,0},{0,4},{12,8},{8,12},{5,1},{1,5},{13,9},{9,13},{6,2},{2,6},{1... | collective-permute-start | bytes 688136 | tf_op jit(solution)/shard_map/ppermute | solution.py:251
  135.8 7.9 %collective-permute-start.20 = (bf16[64,1792]{1,0:T(8,128)(2,1)S(1)}, bf16[64,1792]{1,0:T(8,128)(2,1)S(1)}, u32[]{:S(2)}, u32[]{:S(2)}) collective-permute-start(bf16[64,1792]{1,0:T(8,128)(2,1)S(1)} %add_convert_fusion.3), channel_id=1, source_target_pairs={{4,0},{0,4},{12,8},{8,12},{5,1},{1,5},{13,9},{9,13},{6,2},{2,6},{1... | collective-permute-start | bytes 688136 | tf_op jit(solution)/shard_map/ppermute | solution.py:251
where the time goes:
time: 145 us
  waiting for transfers between devices  57.9 us (40%)
  starting transfers between devices  48.9 us (34%)
  Pallas kernels  37.9 us (26%)
    ppermute x28, waiting for transfers between devices, both(): return tuple((lax.ppermute(x, axis, pairs) for x in halves))  57.9 us
    ppermute x28, starting transfers between devices, both(): return tuple((lax.ppermute(x, axis, pairs) for x in halves))  47.9 us
    pallas_call x4, Pallas kernels, run_expert(): pl.pallas_call(functools.partial(expert_kernel, count, tile_of(hid, 256))...  29.5 us
    pallas_call x1, Pallas kernels, stage(): pl.pallas_call(stage_kernel, out_shape=[pltpu.VMEM(a.shape, a.dtype) for...  4.23 us
  transfers between devices with their start and end apart: 31, of which 13 were waited for; matrix products, arithmetic and copies ran while one was open for 0% of the time, Pallas kernels for 25%

commit v1 on v0

v1 whole, which is shorter than its diff:
```python
import functools

import jax
import jax.numpy as jnp
from jax import lax
from jax.experimental import pallas as pl
from jax.experimental.pallas import tpu as pltpu
from jax.sharding import Mesh
from jax.sharding import PartitionSpec as P


SPAN = 4
SWAP = [(0, 1), (1, 0)]
SENDS = {0: 1}
RETURNS = {}
VMEM = pl.BlockSpec(memory_space=pltpu.VMEM)
SMEM = pl.BlockSpec(memory_space=pltpu.SMEM)
HBM = pl.BlockSpec(memory_space=pltpu.HBM)


def held(x):
    return pltpu.with_memory_space_constraint(x, pltpu.HBM)


def grouped(refs, counts):
    refs, groups = list(refs), []
    for n in counts:
        groups.append(refs[:n])
        refs = refs[n:]
    return groups


def window(pieces, column, tile):
    span = pieces[0].shape[1]
    return pieces[column // span], pl.ds(column % span, tile)


def tile_of(size, most):
    return max(t for t in range(128, most + 1, 128) if size % t == 0)


def steps_to(route, plane, experts):
    if experts & (experts - 1) == 0:
        return route ^ plane
    return lax.rem(route - plane + experts, experts)


def grids(rows):
    return [lax.broadcasted_iota(jnp.int32, (rows, rows), d) for d in range(2)]


def turned(row):
    rows = row.shape[1]
    sub, lane = grids(rows)
    wide = jnp.broadcast_to(row, (rows, rows))
    return jnp.sum(jnp.where(sub == lane, wide, jnp.zeros_like(wide)), axis=1, keepdims=True)


def slots_by_row(row, plane, experts, capacity):
    sub, lane = grids(row.shape[1])
    before = ((turned(row) == row) & (sub < lane)).astype(jnp.int32)
    position = jnp.sum(before, axis=0, keepdims=True)
    return steps_to(row, plane, experts) * capacity + position


def pack_kernel(counts, capacity, plane_ref, routes_ref, tokens_ref, *refs):
    outs, (routes, tokens, sems) = refs[:-3], refs[-3:]
    rows, width = tokens.shape
    half = width // 2
    first = pltpu.make_async_copy(routes_ref, routes, sems.at[2])
    first.start()
    copies = []
    for c in range(2):
        part = pl.ds(c * half, half)
        copies.append(
            pltpu.make_async_copy(tokens_ref.at[:, part], tokens.at[:, part], sems.at[c])
        )
        copies[c].start()
    first.wait()
    experts = len(counts)
    outs = grouped(outs, counts)
    slot = slots_by_row(routes[...], plane_ref[0], experts, capacity)
    every = lax.broadcasted_iota(jnp.int32, (experts * capacity, rows), 0)
    pick = (slot == every).astype(jnp.bfloat16)
    tile = tile_of(half, 512)
    for c in range(0, width, tile):
        if c % half == 0:
            copies[c // half].wait()
        value = jnp.dot(pick, tokens[:, pl.ds(c, tile)], preferred_element_type=jnp.float32)
        value = value.astype(jnp.bfloat16)
        for k in range(experts):
            out, part = window(outs[k], c, tile)
            out[:, part] = value[k * capacity : (k + 1) * capacity]


def pieces_of(counts, rows, width):
    return [jax.ShapeDtypeStruct((rows, width // n), jnp.bfloat16) for n in counts for _ in range(n)]


def pack(plane, routes, tokens, counts, capacity):
    rows, width = tokens.shape
    experts = len(counts)
    outs = pl.pallas_call(
        functools.partial(pack_kernel, counts, capacity),
        out_shape=pieces_of(counts, capacity, width),
        in_specs=[SMEM, HBM, HBM],
        out_specs=[VMEM] * sum(counts),
        scratch_shapes=[
            pltpu.VMEM(routes.shape, routes.dtype),
            pltpu.VMEM(tokens.shape, tokens.dtype),
            pltpu.SemaphoreType.DMA((3,)),
        ],
        cost_estimate=pl.CostEstimate(
            flops=2 * rows * experts * capacity * width,
            bytes_accessed=2 * (rows + experts * capacity) * width,
            transcendentals=0,
        ),
        compiler_params=pltpu.CompilerParams(vmem_limit_bytes=12 << 20),
        name="pack",
    )(plane, held(routes), held(tokens))
    return grouped(outs, counts)


def choose(routes_ref, plane_ref, steps, experts, capacity):
    row = routes_ref[...]
    slot = turned(slots_by_row(row, plane_ref[0], experts, capacity))
    first = lax.broadcasted_iota(jnp.int32, (row.shape[1], capacity), 1)
    picks = [(slot == first + k * capacity).astype(jnp.float32) for k in steps]
    return jnp.concatenate(picks, axis=1).astype(jnp.bfloat16)


def gathered(pick, blocks, column, tile):
    parts = [window(block, column, tile) for block in blocks]
    data = jnp.concatenate([piece[:, part] for piece, part in parts], axis=0)
    return jnp.dot(pick, data, preferred_element_type=jnp.float32)


def write(held, column, tile, out, sem):
    whole, part = pl.ds(column, tile), pl.ds(column % held.shape[1], tile)
    copy = pltpu.make_async_copy(held.at[:, part], out.at[:, whole], sem)
    copy.start()
    return copy


def base_kernel(experts, capacity, early, late, plane_ref, routes_ref, scale_ref, *refs):
    steps, counts = zip(*early)
    more, _ = zip(*late)
    blocks, ends, rest = grouped(refs, (sum(counts), len(late), 6))
    out, base, kept, factor, held, sems = rest
    blocks = grouped(blocks, counts)
    pick = choose(routes_ref, plane_ref, steps, experts, capacity)
    extra = choose(routes_ref, plane_ref, more, experts, capacity)
    scale = turned(scale_ref[...])
    kept[...] = extra
    factor[...] = jnp.broadcast_to(scale, factor.shape)
    half = held.shape[1]
    tile = tile_of(half, 512)
    copies = []
    for n, c in enumerate(range(0, half, tile)):
        value = gathered(pick, blocks, c, tile) + gathered(extra, [[e] for e in ends], c, tile)
        held[:, pl.ds(c, tile)] = (scale * value).astype(held.dtype)
        copies.append(write(held, c, tile, out, sems.at[n]))
    for c in range(0, half, tile):
        base[:, pl.ds(c, tile)] = gathered(pick, blocks, half + c, tile)
    for copy in copies:
        copy.wait()


def final_kernel(pick_ref, scale_ref, base, *refs):
    ends, (_, out, held, sems) = grouped(refs, (len(refs) - 4, 4))
    pick, scale = pick_ref[...], scale_ref[:, :1]
    half = held.shape[1]
    tile = tile_of(half, 512)
    copies = []
    for n, c in enumerate(range(0, half, tile)):
        value = base[:, pl.ds(c, tile)] + gathered(pick, [[e] for e in ends], c, tile)
        held[:, pl.ds(c, tile)] = (scale * value).astype(held.dtype)
        copies.append(write(held, half + c, tile, out, sems.at[n]))
    for copy in copies:
        copy.wait()


def place_left(plane, routes, scale, early, late, experts):
    rows = routes.shape[1]
    capacity, half = late[0][1][0].shape
    blocks = [piece for _, pieces in early for piece in pieces] + [p[0] for _, p in late]
    return pl.pallas_call(
        functools.partial(
            base_kernel,
            experts,
            capacity,
            [(k, len(pieces)) for k, pieces in early],
            [(k, 1) for k, _ in late],
        ),
        out_shape=[
            jax.ShapeDtypeStruct((rows, 2 * half), jnp.bfloat16),
            jax.ShapeDtypeStruct((rows, half), jnp.float32),
            jax.ShapeDtypeStruct((rows, len(late) * capacity), jnp.bfloat16),
            jax.ShapeDtypeStruct((rows, 128), jnp.float32),
        ],
        in_specs=[SMEM] + [VMEM] * (2 + len(blocks)),
        out_specs=[HBM, VMEM, VMEM, VMEM],
        scratch_shapes=[
            pltpu.VMEM((rows, half), jnp.bfloat16),
            pltpu.SemaphoreType.DMA((half // tile_of(half, 512),)),
        ],
        compiler_params=pltpu.CompilerParams(vmem_limit_bytes=12 << 20),
        name="left",
    )(plane, routes, scale, *blocks)


def place_right(out, base, pick, scale, late):
    rows, half = base.shape
    ends = [pieces[1] for _, pieces in late]
    return pl.pallas_call(
        final_kernel,
        out_shape=jax.ShapeDtypeStruct(out.shape, out.dtype),
        in_specs=[VMEM] * (3 + len(ends)) + [HBM],
        out_specs=HBM,
        scratch_shapes=[
            pltpu.VMEM((rows, half), jnp.bfloat16),
            pltpu.SemaphoreType.DMA((half // tile_of(half, 512),)),
        ],
        input_output_aliases={3 + len(ends): 0},
        compiler_params=pltpu.CompilerParams(vmem_limit_bytes=12 << 20),
        name="right",
    )(pick, scale, base, *ends, out)


def stage_kernel(*refs):
    count = (len(refs) - 1) // 2
    sems = refs[-1]
    copies = [
        pltpu.make_async_copy(refs[i], refs[count + i], sems.at[i]) for i in range(count)
    ]
    for copy in copies:
        copy.start()
    for copy in copies:
        copy.wait()


def stage(arrays):
    return pl.pallas_call(
        stage_kernel,
        out_shape=[pltpu.VMEM(a.shape, a.dtype) for a in arrays],
        in_specs=[HBM] * len(arrays),
        out_specs=[VMEM] * len(arrays),
        scratch_shapes=[pltpu.SemaphoreType.DMA((len(arrays),))],
        cost_estimate=pl.CostEstimate(
            flops=0, bytes_accessed=4 * sum(a.size for a in arrays), transcendentals=0
        ),
        compiler_params=pltpu.CompilerParams(vmem_limit_bytes=4 << 20),
        name="stage",
    )(*[held(a) for a in arrays])


def expert_kernel(in_counts, out_counts, hid_tile, *refs):
    ins, weights, outs, scratch = grouped(refs, (sum(in_counts), 6, sum(out_counts), 2))
    rows, hidden = scratch
    ins, outs = grouped(ins, in_counts), grouped(outs, out_counts)
    capacity, width = rows.shape[0] // len(ins), rows.shape[1]
    hid = hidden.shape[1] // 2
    for i, block in enumerate(ins):
        span = width // len(block)
        for c, piece in enumerate(block):
            rows[pl.ds(i * capacity, capacity), pl.ds(c * span, span)] = piece[...]
    x = rows[...]
    for s in range(2):
        gate, up = weights[3 * s], weights[3 * s + 1]
        for h in range(0, hid, hid_tile):
            part = pl.ds(h, hid_tile)
            gate_val = jnp.dot(x, gate[:, part], preferred_element_type=jnp.float32)
            up_val = jnp.dot(x, up[:, part], preferred_element_type=jnp.float32)
            value = gate_val / (1.0 + jnp.exp(-gate_val)) * up_val
            hidden[:, pl.ds(s * hid + h, hid_tile)] = value.astype(jnp.bfloat16)
    tile = tile_of(width // 2, 512)
    for c in range(0, width, tile):
        whole = pl.ds(c, tile)
        value = jnp.dot(hidden[:, :hid], weights[2][:, whole], preferred_element_type=jnp.float32)
        value += jnp.dot(hidden[:, hid:], weights[5][:, whole], preferred_element_type=jnp.float32)
        value = value.astype(jnp.bfloat16)
        for i, block in enumerate(outs):
            out, part = window(block, c, tile)
            out[:, part] = value[i * capacity : (i + 1) * capacity]


def run_expert(blocks, out_counts, weights):
    in_counts = [len(block) for block in blocks]
    capacity, width = blocks[0][0].shape[0], in_counts[0] * blocks[0][0].shape[1]
    total = len(blocks) * capacity
    hid = weights[0].shape[1]
    outs = pl.pallas_call(
        functools.partial(expert_kernel, in_counts, out_counts, tile_of(hid, 256)),
        out_shape=pieces_of(out_counts, capacity, width),
        in_specs=[VMEM] * (sum(in_counts) + 6),
        out_specs=[VMEM] * sum(out_counts),
        scratch_shapes=[
            pltpu.VMEM((total, width), jnp.bfloat16),
            pltpu.VMEM((total, 2 * hid), jnp.bfloat16),
        ],
        compiler_params=pltpu.CompilerParams(vmem_limit_bytes=16 << 20),
        cost_estimate=pl.CostEstimate(
            flops=2 * total * width * hid * 6,
            bytes_accessed=12 * width * hid + 4 * total * width,
            transcendentals=total * hid * 2,
        ),
        name="expert",
    )(*[piece for block in blocks for piece in block], *weights)
    return grouped(outs, out_counts)


def per_device(tokens, routes, gate_weights, w_gate, w_up, w_down):
    rows = tokens.shape[0]
    experts = lax.axis_size("plane")
    capacity = 2 * rows // experts
    paired = experts & (experts - 1) == 0
    plane = jnp.reshape(lax.axis_index("plane"), (1,)).astype(jnp.int32)
    routes, scale = routes.reshape(1, rows), gate_weights.reshape(1, rows)

    def there(k):
        return [(i, i ^ k if paired else (i + k) % experts) for i in range(experts)]

    def back(k):
        return [(b, a) for a, b in there(k)]

    def moves(pieces, axis, pairs):
        return [lax.ppermute(x, axis, pairs) for x in pieces]

    sends = [SENDS.get(k, 2) for k in range(experts)]
    packed = pack(plane, routes, tokens, sends, capacity)
    own = moves(packed[0], "row", SWAP)
    sent = {k: moves(packed[k], "plane", there(k)) for k in range(1, experts)}
    weights = [w_gate[0], w_up[0], w_down[0]]
    other = [lax.ppermute(w, "core", SWAP) for w in weights]
    weights = [*stage(weights), *other]

    own_a, own_b = run_expert([packed[0], own], [1, RETURNS.get(0, 2)], weights)
    items = [(0, own_a), (0, moves(own_b, "row", SWAP))]
    for k in range(1, experts):
        met = moves(sent[k], "row", SWAP)
        count = RETURNS.get(k, 2)
        a, b = run_expert([sent[k], met], [count, count], weights)
        b = moves(b, "row", SWAP)
        total = [
            (u.astype(jnp.float32) + v.astype(jnp.float32)).astype(jnp.bfloat16)
            for u, v in zip(a, b)
        ]
        items.append((k, moves(total, "plane", back(k))))
    early = [items[0]] + items[3:-1]
    late = [items[1], items[2], items[-1]]
    left = place_left(plane, routes, scale, early, late, experts)
    return place_right(*left, late)


def solution(mesh):
    groups, devices = mesh.shape["group"], mesh.shape["expert"]
    experts = devices // SPAN
    fine = Mesh(
        mesh.devices.reshape(groups, experts, SPAN // 2, 2), ("group", "plane", "row", "core")
    )
    every = ("group", "plane", "row", "core")
    expert = ("plane", "row", "core")
    placed = (P(every, None),) * 3 + (P(expert, None, None),) * 3

    return jax.shard_map(
        per_device, mesh=fine, in_specs=placed, out_specs=P(every, None), check_vma=False
    )
```

time: 145 us -> 148 us (1.021)
  the two profiles are of different devices: /device:TPU:0 before, /device:TPU:15 now
where the time goes in v1:
time: 148 us; the launch traced here: 147 us
  waiting for transfers between devices  81.1 us (55%)
  Pallas kernels  38.1 us (26%)
  starting transfers between devices  27 us (18%)
    ppermute x27, waiting for transfers between devices, moves(): return [lax.ppermute(x, axis, pairs) for x in pieces]  81.1 us
    pallas_call x4, Pallas kernels, run_expert(): pl.pallas_call(functools.partial(expert_kernel, in_counts, out_counts, ti...  29.5 us
    ppermute x27, starting transfers between devices, moves(): return [lax.ppermute(x, axis, pairs) for x in pieces]  25.8 us
    pallas_call x1, Pallas kernels, stage(): pl.pallas_call(stage_kernel, out_shape=[pltpu.VMEM(a.shape, a.dtype) for...  4.23 us
  transfers between devices with their start and end apart: 30, of which 17 were waited for; matrix products, arithmetic and copies ran while one was open for 0% of the time, Pallas kernels for 25%

profile of v1, /device:TPU:15, one launch (start us, length us, event | category | flops | bytes accessed | tf_op | source)
XLA Modules:
  0.0 146.9 jit_solution(4220836365805078753)
XLA Ops:
  0.0 0.7 collective-permute-start.1
  0.7 0.0 collective-permute-start.2
  0.7 0.5 collective-permute-start.3
  1.2 1.9 %pack.1 = (bf16[64,3584]{1,0:T(8,128)(2,1)S(1)}, bf16[64,1792]{1,0:T(8,128)(2,1)S(1)}, bf16[64,1792]{1,0:T(8,128)(2,1)S(1)}, bf16[64,1792]{1,0:T(8,128)(2,1)S(1)...) custom-call(s32[1]{0:T(128)} %bitcast.plane_ref, s32[1,128]{1,0:T(1,128)} %bitcast.6, ...), custom_call_target="tpu_custom_call" | custom-call | flops 234881024 | bytes 2752512 | tf_op jit(solution)/shard_map/pack/pallas_call | solution.py:103
  3.1 1.4 collective-permute-start.19
  4.5 0.2 collective-permute-start.20
  4.6 15.5 %collective-permute-done.19.refs_0_ = bf16[64,1792]{1,0:T(8,128)(2,1)S(1)} collective-permute-done((bf16[64,1792]{1,0:T(8,128)(2,1)S(1)}, bf16[64,1792]{1,0:T(8,128)(2,1)S(1)}, u32[]{:S(2)}, u32[]{:S(2)}) %collective-permute-start.19) | collective-permute-done | bytes 229408 | tf_op jit(solution)/shard_map/ppermute | solution.py:327
  20.1 0.0 collective-permute-start.13
  20.1 4.9 %collective-permute-done.20.refs_1_ = bf16[64,1792]{1,0:T(8,128)(2,1)S(1)} collective-permute-done((bf16[64,1792]{1,0:T(8,128)(2,1)S(1)}, bf16[64,1792]{1,0:T(8,128)(2,1)S(1)}, u32[]{:S(2)}, u32[]{:S(2)}) %collective-permute-start.20) | collective-permute-done | bytes 229408 | tf_op jit(solution)/shard_map/ppermute | solution.py:327
  25.1 0.9 collective-permute-done.13.refs_0_
  26.0 1.6 %collective-permute-start.4 = (bf16[64,1792]{1,0:T(8,128)(2,1)S(1)}, bf16[64,1792]{1,0:T(8,128)(2,1)S(1)}, u32[]{:S(2)}, u32[]{:S(2)}) collective-permute-start(bf16[64,1792]{1,0:T(8,128)(2,1)S(1)} %get-tuple-element.39), channel_id=1, source_target_pairs={{0,8},{4,12},{8,0},{12,4},{1,9},{5,13},{9,1},{13,5},{2,10},{6,14},... | collective-permute-start | bytes 688136 | tf_op jit(solution)/shard_map/ppermute | solution.py:327
  27.5 6.2 %collective-permute-done.14.refs_1_ = bf16[64,1792]{1,0:T(8,128)(2,1)S(1)} collective-permute-done((bf16[64,1792]{1,0:T(8,128)(2,1)S(1)}, bf16[64,1792]{1,0:T(8,128)(2,1)S(1)}, u32[]{:S(2)}, u32[]{:S(2)}) %collective-permute-start.14) | collective-permute-done | bytes 229408 | tf_op jit(solution)/shard_map/ppermute | solution.py:327
  33.8 2.6 %collective-permute-start.5 = (bf16[64,1792]{1,0:T(8,128)(2,1)S(1)}, bf16[64,1792]{1,0:T(8,128)(2,1)S(1)}, u32[]{:S(2)}, u32[]{:S(2)}) collective-permute-start(bf16[64,1792]{1,0:T(8,128)(2,1)S(1)} %get-tuple-element.40), channel_id=1, source_target_pairs={{0,8},{4,12},{8,0},{12,4},{1,9},{5,13},{9,1},{13,5},{2,10},{6,14},... | collective-permute-start | bytes 688136 | tf_op jit(solution)/shard_map/ppermute | solution.py:327
  36.3 1.0 collective-permute-done.4.refs_0_
  37.3 0.2 collective-permute-start.21
  37.6 8.9 %collective-permute-done.5.refs_1_ = bf16[64,1792]{1,0:T(8,128)(2,1)S(1)} collective-permute-done((bf16[64,1792]{1,0:T(8,128)(2,1)S(1)}, bf16[64,1792]{1,0:T(8,128)(2,1)S(1)}, u32[]{:S(2)}, u32[]{:S(2)}) %collective-permute-start.5) | collective-permute-done | bytes 229408 | tf_op jit(solution)/shard_map/ppermute | solution.py:327
  46.5 0.2 collective-permute-start.22
  46.7 4.2 %stage.1 = (bf16[3584,512]{1,0:T(8,128)(2,1)S(1)}, bf16[3584,512]{1,0:T(8,128)(2,1)S(1)}, bf16[512,3584]{1,0:T(8,128)(2,1)S(1)}) custom-call(bf16[3584,512]{1,0:T(8,128)(2,1)} %bitcast.10, bf16[3584,512]{1,0:T(8,128)(2,1)} %bitcast.12, bf16[512,3584]{1,0:T(8,128)(2,1)} %bitcast.14), custom_call_target="tpu_custom_call" | custom-call | bytes 22020096 | tf_op jit(solution)/shard_map/stage/pallas_call | solution.py:243
  51.0 1.3 collective-permute-start
  52.3 1.5 %collective-permute-done.22.refs_3_ = bf16[64,1792]{1,0:T(8,128)(2,1)S(1)} collective-permute-done((bf16[64,1792]{1,0:T(8,128)(2,1)S(1)}, bf16[64,1792]{1,0:T(8,128)(2,1)S(1)}, u32[]{:S(2)}, u32[]{:S(2)}) %collective-permute-start.22) | collective-permute-done | bytes 229408 | tf_op jit(solution)/shard_map/ppermute | solution.py:327
  53.8 0.2 collective-permute-start.15
  54.1 1.2 collective-permute-start.16
  55.3 0.0 collective-permute-done.2.refs_6_.refs_8_
  55.3 0.2 collective-permute-start.6
  55.5 0.0 collective-permute-done.3.refs_7_.refs_9_
  55.5 1.2 collective-permute-start.7
  56.8 7.3 %expert.7 = (bf16[64,1792]{1,0:T(8,128)(2,1)S(1)}, bf16[64,1792]{1,0:T(8,128)(2,1)S(1)}, bf16[64,1792]{1,0:T(8,128)(2,1)S(1)}, bf16[64,1792]{1,0:T(8,128)(2,1)S(1)}) custom-call(bf16[64,1792]{1,0:T(8,128)(2,1)S(1)} %collective-permute-done.19.refs_0_, bf16[64,1792]{1,0:T(8,128)(2,1)S(1)} %collective-permute-done.20.refs_1_, ...), custom_call_target="tpu_custom_call" | custom-call | flops 2818572288 | bytes 23855104 | tf_op jit(solution)/shard_map/expert/pallas_call | solution.py:292
  64.1 4.5 %collective-permute-done.15.refs_2_ = bf16[64,1792]{1,0:T(8,128)(2,1)S(1)} collective-permute-done((bf16[64,1792]{1,0:T(8,128)(2,1)S(1)}, bf16[64,1792]{1,0:T(8,128)(2,1)S(1)}, u32[]{:S(2)}, u32[]{:S(2)}) %collective-permute-start.15) | collective-permute-done | bytes 229408 | tf_op jit(solution)/shard_map/ppermute | solution.py:327
  68.6 4.9 %collective-permute-done.16.refs_3_ = bf16[64,1792]{1,0:T(8,128)(2,1)S(1)} collective-permute-done((bf16[64,1792]{1,0:T(8,128)(2,1)S(1)}, bf16[64,1792]{1,0:T(8,128)(2,1)S(1)}, u32[]{:S(2)}, u32[]{:S(2)}) %collective-permute-start.16) | collective-permute-done | bytes 229408 | tf_op jit(solution)/shard_map/ppermute | solution.py:327
  73.5 7.3 %expert.6 = (bf16[64,1792]{1,0:T(8,128)(2,1)S(1)}, bf16[64,1792]{1,0:T(8,128)(2,1)S(1)}, bf16[64,1792]{1,0:T(8,128)(2,1)S(1)}, bf16[64,1792]{1,0:T(8,128)(2,1)S(1)}) custom-call(bf16[64,1792]{1,0:T(8,128)(2,1)S(1)} %collective-permute-done.13.refs_0_, bf16[64,1792]{1,0:T(8,128)(2,1)S(1)} %collective-permute-done.14.refs_1_, ...), custom_call_target="tpu_custom_call" | custom-call | flops 2818572288 | bytes 23855104 | tf_op jit(solution)/shard_map/expert/pallas_call | solution.py:292
  80.8 0.1 collective-permute-start.26
  80.9 0.0 collective-permute-done.6.refs_2_
  80.9 1.4 collective-permute-start.23
  82.4 1.0 collective-permute-done.7.refs_3_
  83.3 7.3 %expert.5 = (bf16[64,1792]{1,0:T(8,128)(2,1)S(1)}, bf16[64,1792]{1,0:T(8,128)(2,1)S(1)}, bf16[64,1792]{1,0:T(8,128)(2,1)S(1)}, bf16[64,1792]{1,0:T(8,128)(2,1)S(1)}) custom-call(bf16[64,1792]{1,0:T(8,128)(2,1)S(1)} %collective-permute-done.4.refs_0_, bf16[64,1792]{1,0:T(8,128)(2,1)S(1)} %collective-permute-done.5.refs_1_, ...), custom_call_target="tpu_custom_call" | custom-call | flops 2818572288 | bytes 23855104 | tf_op jit(solution)/shard_map/expert/pallas_call | solution.py:292
  90.6 0.0 collective-permute-done.refs_1_
  90.7 1.5 %collective-permute-start.10 = (bf16[64,1792]{1,0:T(8,128)(2,1)S(1)}, bf16[64,1792]{1,0:T(8,128)(2,1)S(1)}, u32[]{:S(2)}, u32[]{:S(2)}) collective-permute-start(bf16[64,1792]{1,0:T(8,128)(2,1)S(1)} %get-tuple-element.44), channel_id=1, source_target_pairs={{0,2},{2,0},{1,3},{3,1},{4,6},{6,4},{5,7},{7,5},{8,10},{10,8},{9,1... | collective-permute-start | bytes 688136 | tf_op jit(solution)/shard_map/ppermute | solution.py:327
  92.2 7.5 %expert.4 = (bf16[64,3584]{1,0:T(8,128)(2,1)S(1)}, bf16[64,1792]{1,0:T(8,128)(2,1)S(1)}, bf16[64,1792]{1,0:T(8,128)(2,1)S(1)}) custom-call(bf16[64,3584]{1,0:T(8,128)(2,1)S(1)} %get-tuple-element.34.refs_0_, bf16[64,3584]{1,0:T(8,128)(2,1)S(1)} %collective-permute-done.refs_1_, bf16[3584,512]{1,0:T(8,128)(2,1)S(1)} %get-tuple-element.35.refs_2_.refs_4_, ...), custom_call_target="tpu_custom_call" | custom-call | flops 2818572288 | bytes 23855104 | tf_op jit(solution)/shard_map/expert/pallas_call | solution.py:292
  99.7 0.0 copy-start
  99.7 0.0 copy-start.1
  99.8 0.0 collective-permute-done.28
  99.8 0.1 collective-permute-start.8
  99.8 0.1 add_convert_fusion
  99.9 1.5 %collective-permute-start.12 = (bf16[64,1792]{1,0:T(8,128)(2,1)S(1)}, bf16[64,1792]{1,0:T(8,128)(2,1)S(1)}, u32[]{:S(2)}, u32[]{:S(2)}) collective-permute-start(bf16[64,1792]{1,0:T(8,128)(2,1)S(1)} %get-tuple-element.45), channel_id=1, source_target_pairs={{0,2},{2,0},{1,3},{3,1},{4,6},{6,4},{5,7},{7,5},{8,10},{10,8},{9,1... | collective-permute-start | bytes 688136 | tf_op jit(solution)/shard_map/ppermute | solution.py:327
  101.4 0.1 add_convert_fusion.2
  101.5 1.5 %collective-permute-done.17 = bf16[64,1792]{1,0:T(8,128)(2,1)S(1)} collective-permute-done((bf16[64,1792]{1,0:T(8,128)(2,1)S(1)}, bf16[64,1792]{1,0:T(8,128)(2,1)S(1)}, u32[]{:S(2)}, u32[]{:S(2)}) %collective-permute-start.17) | collective-permute-done | bytes 229408 | tf_op jit(solution)/shard_map/ppermute | solution.py:327
  103.0 0.7 collective-permute-start.24
  103.7 0.1 add_convert_fusion.3
  103.8 4.1 %collective-permute-done.10 = bf16[64,1792]{1,0:T(8,128)(2,1)S(1)} collective-permute-done((bf16[64,1792]{1,0:T(8,128)(2,1)S(1)}, bf16[64,1792]{1,0:T(8,128)(2,1)S(1)}, u32[]{:S(2)}, u32[]{:S(2)}) %collective-permute-start.10) | collective-permute-done | bytes 229408 | tf_op jit(solution)/shard_map/ppermute | solution.py:327
  107.9 2.6 %collective-permute-start.18 = (bf16[64,1792]{1,0:T(8,128)(2,1)S(1)}, bf16[64,1792]{1,0:T(8,128)(2,1)S(1)}, u32[]{:S(2)}, u32[]{:S(2)}) collective-permute-start(bf16[64,1792]{1,0:T(8,128)(2,1)S(1)} %add_convert_fusion.3), channel_id=1, source_target_pairs={{4,0},{0,4},{12,8},{8,12},{5,1},{1,5},{13,9},{9,13},{6,2},{2,6},{1... | collective-permute-start | bytes 688136 | tf_op jit(solution)/shard_map/ppermute | solution.py:327
  110.5 0.1 add_convert_fusion.4
  110.6 2.2 %collective-permute-done.8 = bf16[64,1792]{1,0:T(8,128)(2,1)S(1)} collective-permute-done((bf16[64,1792]{1,0:T(8,128)(2,1)S(1)}, bf16[64,1792]{1,0:T(8,128)(2,1)S(1)}, u32[]{:S(2)}, u32[]{:S(2)}) %collective-permute-start.8) | collective-permute-done | bytes 229408 | tf_op jit(solution)/shard_map/ppermute | solution.py:327
  112.8 3.1 %collective-permute-start.11 = (bf16[64,1792]{1,0:T(8,128)(2,1)S(1)}, bf16[64,1792]{1,0:T(8,128)(2,1)S(1)}, u32[]{:S(2)}, u32[]{:S(2)}) collective-permute-start(bf16[64,1792]{1,0:T(8,128)(2,1)S(1)} %add_convert_fusion.4), channel_id=1, source_target_pairs={{8,0},{12,4},{0,8},{4,12},{9,1},{13,5},{1,9},{5,13},{10,2},{14,6},... | collective-permute-start | bytes 688136 | tf_op jit(solution)/shard_map/ppermute | solution.py:327
  115.9 0.1 add_convert_fusion.5
  116.0 0.1 collective-permute-start.9
  116.1 0.1 add_convert_fusion.1
  116.1 1.6 %collective-permute-done.12.refs_3_ = bf16[64,1792]{1,0:T(8,128)(2,1)S(1)} collective-permute-done((bf16[64,1792]{1,0:T(8,128)(2,1)S(1)}, bf16[64,1792]{1,0:T(8,128)(2,1)S(1)}, u32[]{:S(2)}, u32[]{:S(2)}) %collective-permute-start.12) | collective-permute-done | bytes 229408 | tf_op jit(solution)/shard_map/ppermute | solution.py:327
  117.7 1.2 collective-permute-start.29
  118.9 3.1 %collective-permute-start.27 = (bf16[64,1792]{1,0:T(8,128)(2,1)S(1)}, bf16[64,1792]{1,0:T(8,128)(2,1)S(1)}, u32[]{:S(2)}, u32[]{:S(2)}) collective-permute-start(bf16[64,1792]{1,0:T(8,128)(2,1)S(1)} %add_convert_fusion.1), channel_id=1, source_target_pairs={{4,0},{0,4},{12,8},{8,12},{5,1},{1,5},{13,9},{9,13},{6,2},{2,6},{1... | collective-permute-start | bytes 688136 | tf_op jit(solution)/shard_map/ppermute | solution.py:327
  122.0 10.3 %collective-permute-done.11.refs_2_ = bf16[64,1792]{1,0:T(8,128)(2,1)S(1)} collective-permute-done((bf16[64,1792]{1,0:T(8,128)(2,1)S(1)}, bf16[64,1792]{1,0:T(8,128)(2,1)S(1)}, u32[]{:S(2)}, u32[]{:S(2)}) %collective-permute-start.11) | collective-permute-done | bytes 229408 | tf_op jit(solution)/shard_map/ppermute | solution.py:327
  132.3 6.7 %collective-permute-done.9.refs_1_ = bf16[64,1792]{1,0:T(8,128)(2,1)S(1)} collective-permute-done((bf16[64,1792]{1,0:T(8,128)(2,1)S(1)}, bf16[64,1792]{1,0:T(8,128)(2,1)S(1)}, u32[]{:S(2)}, u32[]{:S(2)}) %collective-permute-start.9) | collective-permute-done | bytes 229408 | tf_op jit(solution)/shard_map/ppermute | solution.py:327
  139.0 1.4 left.1
  140.4 5.4 %collective-permute-done.29.refs_2_ = bf16[64,1792]{1,0:T(8,128)(2,1)S(1)} collective-permute-done((bf16[64,1792]{1,0:T(8,128)(2,1)S(1)}, bf16[64,1792]{1,0:T(8,128)(2,1)S(1)}, u32[]{:S(2)}, u32[]{:S(2)}) %collective-permute-start.29) | collective-permute-done | bytes 229408 | tf_op jit(solution)/shard_map/ppermute | solution.py:327
  145.7 1.0 right.1
  (14 shorter events, 0.0 us)
Async XLA Ops:
  0.0 54.1 %collective-permute-start.1 = (bf16[3584,512]{1,0:T(8,128)(2,1)}, bf16[3584,512]{1,0:T(8,128)(2,1)}, u32[]{:S(2)}, u32[]{:S(2)}) collective-permute-start(bf16[3584,512]{1,0:T(8,128)(2,1)} %bitcast.9), channel_id=1, source_target_pairs={{0,1},{1,0},{2,3},{3,2},{4,5},{5,4},{6,7},{7,6},{8,9},{9,8},{10,11... | collective-permute-start | bytes 11010056 | tf_op jit(solution)/shard_map/ppermute | solution.py:334
  0.7 54.6 %collective-permute-start.2 = (bf16[3584,512]{1,0:T(8,128)(2,1)}, bf16[3584,512]{1,0:T(8,128)(2,1)}, u32[]{:S(2)}, u32[]{:S(2)}) collective-permute-start(bf16[3584,512]{1,0:T(8,128)(2,1)} %bitcast.11), channel_id=1, source_target_pairs={{0,1},{1,0},{2,3},{3,2},{4,5},{5,4},{6,7},{7,6},{8,9},{9,8},{10,11... | collective-permute-start | bytes 11010056 | tf_op jit(solution)/shard_map/ppermute | solution.py:334
  0.7 54.9 %collective-permute-start.3 = (bf16[512,3584]{1,0:T(8,128)(2,1)}, bf16[512,3584]{1,0:T(8,128)(2,1)}, u32[]{:S(2)}, u32[]{:S(2)}) collective-permute-start(bf16[512,3584]{1,0:T(8,128)(2,1)} %bitcast.13), channel_id=1, source_target_pairs={{0,1},{1,0},{2,3},{3,2},{4,5},{5,4},{6,7},{7,6},{8,9},{9,8},{10,11... | collective-permute-start | bytes 11010056 | tf_op jit(solution)/shard_map/ppermute | solution.py:334
  3.1 17.0 %collective-permute-start.19 = (bf16[64,1792]{1,0:T(8,128)(2,1)S(1)}, bf16[64,1792]{1,0:T(8,128)(2,1)S(1)}, u32[]{:S(2)}, u32[]{:S(2)}) collective-permute-start(bf16[64,1792]{1,0:T(8,128)(2,1)S(1)} %get-tuple-element.50), channel_id=1, source_target_pairs={{0,12},{4,8},{8,4},{12,0},{1,13},{5,9},{9,5},{13,1},{2,14},{6,10},... | collective-permute-start | bytes 688136 | tf_op jit(solution)/shard_map/ppermute | solution.py:327
  4.5 20.6 %collective-permute-start.20 = (bf16[64,1792]{1,0:T(8,128)(2,1)S(1)}, bf16[64,1792]{1,0:T(8,128)(2,1)S(1)}, u32[]{:S(2)}, u32[]{:S(2)}) collective-permute-start(bf16[64,1792]{1,0:T(8,128)(2,1)S(1)} %get-tuple-element.51), channel_id=1, source_target_pairs={{0,12},{4,8},{8,4},{12,0},{1,13},{5,9},{9,5},{13,1},{2,14},{6,10},... | collective-permute-start | bytes 688136 | tf_op jit(solution)/shard_map/ppermute | solution.py:327
  20.1 5.8 %collective-permute-start.13 = (bf16[64,1792]{1,0:T(8,128)(2,1)S(1)}, bf16[64,1792]{1,0:T(8,128)(2,1)S(1)}, u32[]{:S(2)}, u32[]{:S(2)}) collective-permute-start(bf16[64,1792]{1,0:T(8,128)(2,1)S(1)} %get-tuple-element.46), channel_id=1, source_target_pairs={{0,4},{4,0},{8,12},{12,8},{1,5},{5,1},{9,13},{13,9},{2,6},{6,2},{1... | collective-permute-start | bytes 688136 | tf_op jit(solution)/shard_map/ppermute | solution.py:327
  25.1 8.7 %collective-permute-start.14 = (bf16[64,1792]{1,0:T(8,128)(2,1)S(1)}, bf16[64,1792]{1,0:T(8,128)(2,1)S(1)}, u32[]{:S(2)}, u32[]{:S(2)}) collective-permute-start(bf16[64,1792]{1,0:T(8,128)(2,1)S(1)} %get-tuple-element.47), channel_id=1, source_target_pairs={{0,4},{4,0},{8,12},{12,8},{1,5},{5,1},{9,13},{13,9},{2,6},{6,2},{1... | collective-permute-start | bytes 688136 | tf_op jit(solution)/shard_map/ppermute | solution.py:327
  26.0 11.4 %collective-permute-start.4 = (bf16[64,1792]{1,0:T(8,128)(2,1)S(1)}, bf16[64,1792]{1,0:T(8,128)(2,1)S(1)}, u32[]{:S(2)}, u32[]{:S(2)}) collective-permute-start(bf16[64,1792]{1,0:T(8,128)(2,1)S(1)} %get-tuple-element.39), channel_id=1, source_target_pairs={{0,8},{4,12},{8,0},{12,4},{1,9},{5,13},{9,1},{13,5},{2,10},{6,14},... | collective-permute-start | bytes 688136 | tf_op jit(solution)/shard_map/ppermute | solution.py:327
  33.8 12.7 %collective-permute-start.5 = (bf16[64,1792]{1,0:T(8,128)(2,1)S(1)}, bf16[64,1792]{1,0:T(8,128)(2,1)S(1)}, u32[]{:S(2)}, u32[]{:S(2)}) collective-permute-start(bf16[64,1792]{1,0:T(8,128)(2,1)S(1)} %get-tuple-element.40), channel_id=1, source_target_pairs={{0,8},{4,12},{8,0},{12,4},{1,9},{5,13},{9,1},{13,5},{2,10},{6,14},... | collective-permute-start | bytes 688136 | tf_op jit(solution)/shard_map/ppermute | solution.py:327
  37.3 13.6 %collective-permute-start.21 = (bf16[64,1792]{1,0:T(8,128)(2,1)S(1)}, bf16[64,1792]{1,0:T(8,128)(2,1)S(1)}, u32[]{:S(2)}, u32[]{:S(2)}) collective-permute-start(bf16[64,1792]{1,0:T(8,128)(2,1)S(1)} %collective-permute-done.19.refs_0_), channel_id=1, source_target_pairs={{0,2},{2,0},{1,3},{3,1},{4,6},{6,4},{5,7},{7,5},{8,10},{10,8},{9,1... | collective-permute-start | bytes 688136 | tf_op jit(solution)/shard_map/ppermute | solution.py:327
  46.5 7.3 %collective-permute-start.22 = (bf16[64,1792]{1,0:T(8,128)(2,1)S(1)}, bf16[64,1792]{1,0:T(8,128)(2,1)S(1)}, u32[]{:S(2)}, u32[]{:S(2)}) collective-permute-start(bf16[64,1792]{1,0:T(8,128)(2,1)S(1)} %collective-permute-done.20.refs_1_), channel_id=1, source_target_pairs={{0,2},{2,0},{1,3},{3,1},{4,6},{6,4},{5,7},{7,5},{8,10},{10,8},{9,1... | collective-permute-start | bytes 688136 | tf_op jit(solution)/shard_map/ppermute | solution.py:327
  51.0 39.7 %collective-permute-start = (bf16[64,3584]{1,0:T(8,128)(2,1)S(1)}, bf16[64,3584]{1,0:T(8,128)(2,1)S(1)}, u32[]{:S(2)}, u32[]{:S(2)}) collective-permute-start(bf16[64,3584]{1,0:T(8,128)(2,1)S(1)} %get-tuple-element.34.refs_0_), channel_id=1, source_target_pairs={{0,2},{2,0},{1,3},{3,1},{4,6},{6,4},{5,7},{7,5},{8,10},{10,8},{9,1... | collective-permute-start | bytes 1376264 | tf_op jit(solution)/shard_map/ppermute | solution.py:327
  53.8 14.7 %collective-permute-start.15 = (bf16[64,1792]{1,0:T(8,128)(2,1)S(1)}, bf16[64,1792]{1,0:T(8,128)(2,1)S(1)}, u32[]{:S(2)}, u32[]{:S(2)}) collective-permute-start(bf16[64,1792]{1,0:T(8,128)(2,1)S(1)} %collective-permute-done.13.refs_0_), channel_id=1, source_target_pairs={{0,2},{2,0},{1,3},{3,1},{4,6},{6,4},{5,7},{7,5},{8,10},{10,8},{9,1... | collective-permute-start | bytes 688136 | tf_op jit(solution)/shard_map/ppermute | solution.py:327
  54.1 19.4 %collective-permute-start.16 = (bf16[64,1792]{1,0:T(8,128)(2,1)S(1)}, bf16[64,1792]{1,0:T(8,128)(2,1)S(1)}, u32[]{:S(2)}, u32[]{:S(2)}) collective-permute-start(bf16[64,1792]{1,0:T(8,128)(2,1)S(1)} %collective-permute-done.14.refs_1_), channel_id=1, source_target_pairs={{0,2},{2,0},{1,3},{3,1},{4,6},{6,4},{5,7},{7,5},{8,10},{10,8},{9,1... | collective-permute-start | bytes 688136 | tf_op jit(solution)/shard_map/ppermute | solution.py:327
  55.3 25.6 %collective-permute-start.6 = (bf16[64,1792]{1,0:T(8,128)(2,1)S(1)}, bf16[64,1792]{1,0:T(8,128)(2,1)S(1)}, u32[]{:S(2)}, u32[]{:S(2)}) collective-permute-start(bf16[64,1792]{1,0:T(8,128)(2,1)S(1)} %collective-permute-done.4.refs_0_), channel_id=1, source_target_pairs={{0,2},{2,0},{1,3},{3,1},{4,6},{6,4},{5,7},{7,5},{8,10},{10,8},{9,1... | collective-permute-start | bytes 688136 | tf_op jit(solution)/shard_map/ppermute | solution.py:327
  55.5 27.8 %collective-permute-start.7 = (bf16[64,1792]{1,0:T(8,128)(2,1)S(1)}, bf16[64,1792]{1,0:T(8,128)(2,1)S(1)}, u32[]{:S(2)}, u32[]{:S(2)}) collective-permute-start(bf16[64,1792]{1,0:T(8,128)(2,1)S(1)} %collective-permute-done.5.refs_1_), channel_id=1, source_target_pairs={{0,2},{2,0},{1,3},{3,1},{4,6},{6,4},{5,7},{7,5},{8,10},{10,8},{9,1... | collective-permute-start | bytes 688136 | tf_op jit(solution)/shard_map/ppermute | solution.py:327
  68.6 31.2 %collective-permute-start.28 = (bf16[64,1792]{1,0:T(8,128)(2,1)S(1)}, bf16[64,1792]{1,0:T(8,128)(2,1)S(1)}, u32[]{:S(2)}, u32[]{:S(2)}) collective-permute-start(bf16[64,1792]{1,0:T(8,128)(2,1)S(1)} %get-tuple-element.61), channel_id=1, source_target_pairs={{0,2},{2,0},{1,3},{3,1},{4,6},{6,4},{5,7},{7,5},{8,10},{10,8},{9,1... | collective-permute-start | bytes 688136 | tf_op jit(solution)/shard_map/ppermute | solution.py:327
  80.8 35.1 %collective-permute-start.26 = (bf16[64,1792]{1,0:T(8,128)(2,1)S(1)}, bf16[64,1792]{1,0:T(8,128)(2,1)S(1)}, u32[]{:S(2)}, u32[]{:S(2)}) collective-permute-start(bf16[64,1792]{1,0:T(8,128)(2,1)S(1)} %get-tuple-element.59), channel_id=1, source_target_pairs={{0,2},{2,0},{1,3},{3,1},{4,6},{6,4},{5,7},{7,5},{8,10},{10,8},{9,1... | collective-permute-start | bytes 688136 | tf_op jit(solution)/shard_map/ppermute | solution.py:327
  80.9 19.0 %collective-permute-start.23 = (bf16[64,1792]{1,0:T(8,128)(2,1)S(1)}, bf16[64,1792]{1,0:T(8,128)(2,1)S(1)}, u32[]{:S(2)}, u32[]{:S(2)}) collective-permute-start(bf16[64,1792]{1,0:T(8,128)(2,1)S(1)} %get-tuple-element.53), channel_id=1, source_target_pairs={{0,2},{2,0},{1,3},{3,1},{4,6},{6,4},{5,7},{7,5},{8,10},{10,8},{9,1... | collective-permute-start | bytes 688136 | tf_op jit(solution)/shard_map/ppermute | solution.py:327
  83.3 19.7 %collective-permute-start.17 = (bf16[64,1792]{1,0:T(8,128)(2,1)S(1)}, bf16[64,1792]{1,0:T(8,128)(2,1)S(1)}, u32[]{:S(2)}, u32[]{:S(2)}) collective-permute-start(bf16[64,1792]{1,0:T(8,128)(2,1)S(1)} %get-tuple-element.49), channel_id=1, source_target_pairs={{0,2},{2,0},{1,3},{3,1},{4,6},{6,4},{5,7},{7,5},{8,10},{10,8},{9,1... | collective-permute-start | bytes 688136 | tf_op jit(solution)/shard_map/ppermute | solution.py:327
  90.7 17.2 %collective-permute-start.10 = (bf16[64,1792]{1,0:T(8,128)(2,1)S(1)}, bf16[64,1792]{1,0:T(8,128)(2,1)S(1)}, u32[]{:S(2)}, u32[]{:S(2)}) collective-permute-start(bf16[64,1792]{1,0:T(8,128)(2,1)S(1)} %get-tuple-element.44), channel_id=1, source_target_pairs={{0,2},{2,0},{1,3},{3,1},{4,6},{6,4},{5,7},{7,5},{8,10},{10,8},{9,1... | collective-permute-start | bytes 688136 | tf_op jit(solution)/shard_map/ppermute | solution.py:327
  99.7 39.2 %copy-start = (s32[128,1]{0,1:T(1,128)S(1)}, s32[128,1]{0,1:T(1,128)}, u32[]{:S(2)}) copy-start(s32[128,1]{0,1:T(1,128)} %param.7) | copy-start | bytes 1540
  99.7 39.2 %copy-start.1 = (f32[128,1]{0,1:T(1,128)S(1)}, f32[128,1]{0,1:T(1,128)}, u32[]{:S(2)}) copy-start(f32[128,1]{0,1:T(1,128)} %param.8) | copy-start | bytes 1540
  99.8 13.0 %collective-permute-start.8 = (bf16[64,1792]{1,0:T(8,128)(2,1)S(1)}, bf16[64,1792]{1,0:T(8,128)(2,1)S(1)}, u32[]{:S(2)}, u32[]{:S(2)}) collective-permute-start(bf16[64,1792]{1,0:T(8,128)(2,1)S(1)} %get-tuple-element.42), channel_id=1, source_target_pairs={{0,2},{2,0},{1,3},{3,1},{4,6},{6,4},{5,7},{7,5},{8,10},{10,8},{9,1... | collective-permute-start | bytes 688136 | tf_op jit(solution)/shard_map/ppermute | solution.py:327
  99.9 17.8 %collective-permute-start.12 = (bf16[64,1792]{1,0:T(8,128)(2,1)S(1)}, bf16[64,1792]{1,0:T(8,128)(2,1)S(1)}, u32[]{:S(2)}, u32[]{:S(2)}) collective-permute-start(bf16[64,1792]{1,0:T(8,128)(2,1)S(1)} %get-tuple-element.45), channel_id=1, source_target_pairs={{0,2},{2,0},{1,3},{3,1},{4,6},{6,4},{5,7},{7,5},{8,10},{10,8},{9,1... | collective-permute-start | bytes 688136 | tf_op jit(solution)/shard_map/ppermute | solution.py:327
  103.0 14.8 %collective-permute-start.24 = (bf16[64,1792]{1,0:T(8,128)(2,1)S(1)}, bf16[64,1792]{1,0:T(8,128)(2,1)S(1)}, u32[]{:S(2)}, u32[]{:S(2)}) collective-permute-start(bf16[64,1792]{1,0:T(8,128)(2,1)S(1)} %add_convert_fusion.2), channel_id=1, source_target_pairs={{12,0},{8,4},{4,8},{0,12},{13,1},{9,5},{5,9},{1,13},{14,2},{10,6},... | collective-permute-start | bytes 688136 | tf_op jit(solution)/shard_map/ppermute | solution.py:327
  107.9 11.1 %collective-permute-start.18 = (bf16[64,1792]{1,0:T(8,128)(2,1)S(1)}, bf16[64,1792]{1,0:T(8,128)(2,1)S(1)}, u32[]{:S(2)}, u32[]{:S(2)}) collective-permute-start(bf16[64,1792]{1,0:T(8,128)(2,1)S(1)} %add_convert_fusion.3), channel_id=1, source_target_pairs={{4,0},{0,4},{12,8},{8,12},{5,1},{1,5},{13,9},{9,13},{6,2},{2,6},{1... | collective-permute-start | bytes 688136 | tf_op jit(solution)/shard_map/ppermute | solution.py:327
  112.8 19.5 %collective-permute-start.11 = (bf16[64,1792]{1,0:T(8,128)(2,1)S(1)}, bf16[64,1792]{1,0:T(8,128)(2,1)S(1)}, u32[]{:S(2)}, u32[]{:S(2)}) collective-permute-start(bf16[64,1792]{1,0:T(8,128)(2,1)S(1)} %add_convert_fusion.4), channel_id=1, source_target_pairs={{8,0},{12,4},{0,8},{4,12},{9,1},{13,5},{1,9},{5,13},{10,2},{14,6},... | collective-permute-start | bytes 688136 | tf_op jit(solution)/shard_map/ppermute | solution.py:327
  116.0 23.0 %collective-permute-start.9 = (bf16[64,1792]{1,0:T(8,128)(2,1)S(1)}, bf16[64,1792]{1,0:T(8,128)(2,1)S(1)}, u32[]{:S(2)}, u32[]{:S(2)}) collective-permute-start(bf16[64,1792]{1,0:T(8,128)(2,1)S(1)} %add_convert_fusion.5), channel_id=1, source_target_pairs={{8,0},{12,4},{0,8},{4,12},{9,1},{13,5},{1,9},{5,13},{10,2},{14,6},... | collective-permute-start | bytes 688136 | tf_op jit(solution)/shard_map/ppermute | solution.py:327
  117.7 22.7 %collective-permute-start.25 = (bf16[64,1792]{1,0:T(8,128)(2,1)S(1)}, bf16[64,1792]{1,0:T(8,128)(2,1)S(1)}, u32[]{:S(2)}, u32[]{:S(2)}) collective-permute-start(bf16[64,1792]{1,0:T(8,128)(2,1)S(1)} %get-tuple-element.57), channel_id=1, source_target_pairs={{0,2},{2,0},{1,3},{3,1},{4,6},{6,4},{5,7},{7,5},{8,10},{10,8},{9,1... | collective-permute-start | bytes 688136 | tf_op jit(solution)/shard_map/ppermute | solution.py:327
  117.7 28.0 %collective-permute-start.29 = (bf16[64,1792]{1,0:T(8,128)(2,1)S(1)}, bf16[64,1792]{1,0:T(8,128)(2,1)S(1)}, u32[]{:S(2)}, u32[]{:S(2)}) collective-permute-start(bf16[64,1792]{1,0:T(8,128)(2,1)S(1)} %add_convert_fusion), channel_id=1, source_target_pairs={{12,0},{8,4},{4,8},{0,12},{13,1},{9,5},{5,9},{1,13},{14,2},{10,6},... | collective-permute-start | bytes 688136 | tf_op jit(solution)/shard_map/ppermute | solution.py:327
  118.9 26.8 %collective-permute-start.27 = (bf16[64,1792]{1,0:T(8,128)(2,1)S(1)}, bf16[64,1792]{1,0:T(8,128)(2,1)S(1)}, u32[]{:S(2)}, u32[]{:S(2)}) collective-permute-start(bf16[64,1792]{1,0:T(8,128)(2,1)S(1)} %add_convert_fusion.1), channel_id=1, source_target_pairs={{4,0},{0,4},{12,8},{8,12},{5,1},{1,5},{13,9},{9,13},{6,2},{2,6},{1... | collective-permute-start | bytes 688136 | tf_op jit(solution)/shard_map/ppermute | solution.py:327

commit v2 on v1

--- a/solution.py
+++ b/solution.py
@@ -67,14 +67,14 @@
     outs, (routes, tokens, sems) = refs[:-3], refs[-3:]
     rows, width = tokens.shape
     half = width // 2
-    first = pltpu.make_async_copy(routes_ref, routes, sems.at[2])
+    first = pltpu.make_async_copy(routes_ref, routes, sems.at[4])
     first.start()
-    copies = []
-    for c in range(2):
-        part = pl.ds(c * half, half)
-        copies.append(
-            pltpu.make_async_copy(tokens_ref.at[:, part], tokens.at[:, part], sems.at[c])
-        )
+    tile = tile_of(half, 512)
+    copies = {}
+    for n, c in enumerate((0, tile, half, half + 3 * tile)):
+        end = (tile, half, half + 3 * tile, width)[n]
+        part = pl.ds(c, end - c)
+        copies[c] = pltpu.make_async_copy(tokens_ref.at[:, part], tokens.at[:, part], sems.at[n])
         copies[c].start()
     first.wait()
     experts = len(counts)
@@ -84,8 +84,8 @@
     pick = (slot == every).astype(jnp.bfloat16)
     tile = tile_of(half, 512)
     for c in range(0, width, tile):
-        if c % half == 0:
-            copies[c // half].wait()
+        if c in copies:
+            copies[c].wait()
         value = jnp.dot(pick, tokens[:, pl.ds(c, tile)], preferred_element_type=jnp.float32)
         value = value.astype(jnp.bfloat16)
         for k in range(experts):
@@ -108,7 +108,7 @@
         scratch_shapes=[
             pltpu.VMEM(routes.shape, routes.dtype),
             pltpu.VMEM(tokens.shape, tokens.dtype),
-            pltpu.SemaphoreType.DMA((3,)),
+            pltpu.SemaphoreType.DMA((5,)),
         ],
         cost_estimate=pl.CostEstimate(
             flops=2 * rows * experts * capacity * width,

time: 148 us -> 149 us (level)
  no operation moved by 1% of the time
where the time goes in v2:
time: 149 us; the launch traced here: 147 us
  waiting for transfers between devices  81.2 us (54%)
  Pallas kernels  38.2 us (26%)
  starting transfers between devices  27 us (18%)
    ppermute x27, waiting for transfers between devices, moves(): return [lax.ppermute(x, axis, pairs) for x in pieces]  81.2 us
    pallas_call x4, Pallas kernels, run_expert(): pl.pallas_call(functools.partial(expert_kernel, in_counts, out_counts, ti...  29.5 us
    ppermute x27, starting transfers between devices, moves(): return [lax.ppermute(x, axis, pairs) for x in pieces]  25.8 us
    pallas_call x1, Pallas kernels, stage(): pl.pallas_call(stage_kernel, out_shape=[pltpu.VMEM(a.shape, a.dtype) for...  4.23 us
  transfers between devices with their start and end apart: 30, of which 17 were waited for; matrix products, arithmetic and copies ran while one was open for 0% of the time, Pallas kernels for 25%

profile of v2, /device:TPU:15, one launch (start us, length us, event | category | flops | bytes accessed | tf_op | source)
XLA Modules:
  0.0 147.0 jit_solution(5801017808778358537)
XLA Ops:
  0.0 0.7 collective-permute-start.1
  0.7 0.0 collective-permute-start.2
  0.7 0.5 collective-permute-start.3
  1.2 2.0 %pack.1 = (bf16[64,3584]{1,0:T(8,128)(2,1)S(1)}, bf16[64,1792]{1,0:T(8,128)(2,1)S(1)}, bf16[64,1792]{1,0:T(8,128)(2,1)S(1)}, bf16[64,1792]{1,0:T(8,128)(2,1)S(1)...) custom-call(s32[1]{0:T(128)} %bitcast.plane_ref, s32[1,128]{1,0:T(1,128)} %bitcast.6, ...), custom_call_target="tpu_custom_call" | custom-call | flops 234881024 | bytes 2752512 | tf_op jit(solution)/shard_map/pack/pallas_call | solution.py:103
  3.2 1.4 collective-permute-start.19
  4.6 0.2 collective-permute-start.20
  4.7 15.5 %collective-permute-done.19.refs_0_ = bf16[64,1792]{1,0:T(8,128)(2,1)S(1)} collective-permute-done((bf16[64,1792]{1,0:T(8,128)(2,1)S(1)}, bf16[64,1792]{1,0:T(8,128)(2,1)S(1)}, u32[]{:S(2)}, u32[]{:S(2)}) %collective-permute-start.19) | collective-permute-done | bytes 229408 | tf_op jit(solution)/shard_map/ppermute | solution.py:327
  20.3 4.9 %collective-permute-done.20.refs_1_ = bf16[64,1792]{1,0:T(8,128)(2,1)S(1)} collective-permute-done((bf16[64,1792]{1,0:T(8,128)(2,1)S(1)}, bf16[64,1792]{1,0:T(8,128)(2,1)S(1)}, u32[]{:S(2)}, u32[]{:S(2)}) %collective-permute-start.20) | collective-permute-done | bytes 229408 | tf_op jit(solution)/shard_map/ppermute | solution.py:327
  25.2 0.0 collective-permute-start.14
  25.2 0.9 collective-permute-done.13.refs_0_
  26.1 1.5 %collective-permute-start.4 = (bf16[64,1792]{1,0:T(8,128)(2,1)S(1)}, bf16[64,1792]{1,0:T(8,128)(2,1)S(1)}, u32[]{:S(2)}, u32[]{:S(2)}) collective-permute-start(bf16[64,1792]{1,0:T(8,128)(2,1)S(1)} %get-tuple-element.39), channel_id=1, source_target_pairs={{0,8},{4,12},{8,0},{12,4},{1,9},{5,13},{9,1},{13,5},{2,10},{6,14},... | collective-permute-start | bytes 688136 | tf_op jit(solution)/shard_map/ppermute | solution.py:327
  27.7 6.3 %collective-permute-done.14.refs_1_ = bf16[64,1792]{1,0:T(8,128)(2,1)S(1)} collective-permute-done((bf16[64,1792]{1,0:T(8,128)(2,1)S(1)}, bf16[64,1792]{1,0:T(8,128)(2,1)S(1)}, u32[]{:S(2)}, u32[]{:S(2)}) %collective-permute-start.14) | collective-permute-done | bytes 229408 | tf_op jit(solution)/shard_map/ppermute | solution.py:327
  33.9 2.5 %collective-permute-start.5 = (bf16[64,1792]{1,0:T(8,128)(2,1)S(1)}, bf16[64,1792]{1,0:T(8,128)(2,1)S(1)}, u32[]{:S(2)}, u32[]{:S(2)}) collective-permute-start(bf16[64,1792]{1,0:T(8,128)(2,1)S(1)} %get-tuple-element.40), channel_id=1, source_target_pairs={{0,8},{4,12},{8,0},{12,4},{1,9},{5,13},{9,1},{13,5},{2,10},{6,14},... | collective-permute-start | bytes 688136 | tf_op jit(solution)/shard_map/ppermute | solution.py:327
  36.5 1.0 collective-permute-done.4.refs_0_
  37.5 0.2 collective-permute-start.21
  37.7 8.9 %collective-permute-done.5.refs_1_ = bf16[64,1792]{1,0:T(8,128)(2,1)S(1)} collective-permute-done((bf16[64,1792]{1,0:T(8,128)(2,1)S(1)}, bf16[64,1792]{1,0:T(8,128)(2,1)S(1)}, u32[]{:S(2)}, u32[]{:S(2)}) %collective-permute-start.5) | collective-permute-done | bytes 229408 | tf_op jit(solution)/shard_map/ppermute | solution.py:327
  46.6 0.2 collective-permute-start.22
  46.9 4.2 %stage.1 = (bf16[3584,512]{1,0:T(8,128)(2,1)S(1)}, bf16[3584,512]{1,0:T(8,128)(2,1)S(1)}, bf16[512,3584]{1,0:T(8,128)(2,1)S(1)}) custom-call(bf16[3584,512]{1,0:T(8,128)(2,1)} %bitcast.10, bf16[3584,512]{1,0:T(8,128)(2,1)} %bitcast.12, bf16[512,3584]{1,0:T(8,128)(2,1)} %bitcast.14), custom_call_target="tpu_custom_call" | custom-call | bytes 22020096 | tf_op jit(solution)/shard_map/stage/pallas_call | solution.py:243
  51.1 0.0 collective-permute-done.21.refs_2_
  51.1 1.3 collective-permute-start
  52.4 1.5 %collective-permute-done.22.refs_3_ = bf16[64,1792]{1,0:T(8,128)(2,1)S(1)} collective-permute-done((bf16[64,1792]{1,0:T(8,128)(2,1)S(1)}, bf16[64,1792]{1,0:T(8,128)(2,1)S(1)}, u32[]{:S(2)}, u32[]{:S(2)}) %collective-permute-start.22) | collective-permute-done | bytes 229408 | tf_op jit(solution)/shard_map/ppermute | solution.py:327
  53.9 0.2 collective-permute-start.15
  54.2 0.0 collective-permute-done.1.refs_5_.refs_7_
  54.2 1.2 collective-permute-start.16
  55.4 0.0 collective-permute-done.2.refs_6_.refs_8_
  55.4 0.2 collective-permute-start.6
  55.6 0.0 collective-permute-done.3.refs_7_.refs_9_
  55.6 1.2 collective-permute-start.7
  56.9 7.3 %expert.7 = (bf16[64,1792]{1,0:T(8,128)(2,1)S(1)}, bf16[64,1792]{1,0:T(8,128)(2,1)S(1)}, bf16[64,1792]{1,0:T(8,128)(2,1)S(1)}, bf16[64,1792]{1,0:T(8,128)(2,1)S(1)}) custom-call(bf16[64,1792]{1,0:T(8,128)(2,1)S(1)} %collective-permute-done.19.refs_0_, bf16[64,1792]{1,0:T(8,128)(2,1)S(1)} %collective-permute-done.20.refs_1_, ...), custom_call_target="tpu_custom_call" | custom-call | flops 2818572288 | bytes 23855104 | tf_op jit(solution)/shard_map/expert/pallas_call | solution.py:292
  64.2 4.5 %collective-permute-done.15.refs_2_ = bf16[64,1792]{1,0:T(8,128)(2,1)S(1)} collective-permute-done((bf16[64,1792]{1,0:T(8,128)(2,1)S(1)}, bf16[64,1792]{1,0:T(8,128)(2,1)S(1)}, u32[]{:S(2)}, u32[]{:S(2)}) %collective-permute-start.15) | collective-permute-done | bytes 229408 | tf_op jit(solution)/shard_map/ppermute | solution.py:327
  68.7 4.9 %collective-permute-done.16.refs_3_ = bf16[64,1792]{1,0:T(8,128)(2,1)S(1)} collective-permute-done((bf16[64,1792]{1,0:T(8,128)(2,1)S(1)}, bf16[64,1792]{1,0:T(8,128)(2,1)S(1)}, u32[]{:S(2)}, u32[]{:S(2)}) %collective-permute-start.16) | collective-permute-done | bytes 229408 | tf_op jit(solution)/shard_map/ppermute | solution.py:327
  73.6 7.3 %expert.6 = (bf16[64,1792]{1,0:T(8,128)(2,1)S(1)}, bf16[64,1792]{1,0:T(8,128)(2,1)S(1)}, bf16[64,1792]{1,0:T(8,128)(2,1)S(1)}, bf16[64,1792]{1,0:T(8,128)(2,1)S(1)}) custom-call(bf16[64,1792]{1,0:T(8,128)(2,1)S(1)} %collective-permute-done.13.refs_0_, bf16[64,1792]{1,0:T(8,128)(2,1)S(1)} %collective-permute-done.14.refs_1_, ...), custom_call_target="tpu_custom_call" | custom-call | flops 2818572288 | bytes 23855104 | tf_op jit(solution)/shard_map/expert/pallas_call | solution.py:292
  80.9 0.1 collective-permute-start.26
  81.0 1.4 collective-permute-start.23
  82.5 1.0 collective-permute-done.7.refs_3_
  83.4 7.3 %expert.5 = (bf16[64,1792]{1,0:T(8,128)(2,1)S(1)}, bf16[64,1792]{1,0:T(8,128)(2,1)S(1)}, bf16[64,1792]{1,0:T(8,128)(2,1)S(1)}, bf16[64,1792]{1,0:T(8,128)(2,1)S(1)}) custom-call(bf16[64,1792]{1,0:T(8,128)(2,1)S(1)} %collective-permute-done.4.refs_0_, bf16[64,1792]{1,0:T(8,128)(2,1)S(1)} %collective-permute-done.5.refs_1_, ...), custom_call_target="tpu_custom_call" | custom-call | flops 2818572288 | bytes 23855104 | tf_op jit(solution)/shard_map/expert/pallas_call | solution.py:292
  90.8 1.5 %collective-permute-start.10 = (bf16[64,1792]{1,0:T(8,128)(2,1)S(1)}, bf16[64,1792]{1,0:T(8,128)(2,1)S(1)}, u32[]{:S(2)}, u32[]{:S(2)}) collective-permute-start(bf16[64,1792]{1,0:T(8,128)(2,1)S(1)} %get-tuple-element.44), channel_id=1, source_target_pairs={{0,2},{2,0},{1,3},{3,1},{4,6},{6,4},{5,7},{7,5},{8,10},{10,8},{9,1... | collective-permute-start | bytes 688136 | tf_op jit(solution)/shard_map/ppermute | solution.py:327
  92.3 7.5 %expert.4 = (bf16[64,3584]{1,0:T(8,128)(2,1)S(1)}, bf16[64,1792]{1,0:T(8,128)(2,1)S(1)}, bf16[64,1792]{1,0:T(8,128)(2,1)S(1)}) custom-call(bf16[64,3584]{1,0:T(8,128)(2,1)S(1)} %get-tuple-element.34.refs_0_, bf16[64,3584]{1,0:T(8,128)(2,1)S(1)} %collective-permute-done.refs_1_, bf16[3584,512]{1,0:T(8,128)(2,1)S(1)} %get-tuple-element.35.refs_2_.refs_4_, ...), custom_call_target="tpu_custom_call" | custom-call | flops 2818572288 | bytes 23855104 | tf_op jit(solution)/shard_map/expert/pallas_call | solution.py:292
  99.9 0.0 copy-start
  99.9 0.0 copy-start.1
  99.9 0.1 collective-permute-start.8
  100.0 0.1 add_convert_fusion
  100.0 0.0 collective-permute-done.23
  100.0 1.5 %collective-permute-start.12 = (bf16[64,1792]{1,0:T(8,128)(2,1)S(1)}, bf16[64,1792]{1,0:T(8,128)(2,1)S(1)}, u32[]{:S(2)}, u32[]{:S(2)}) collective-permute-start(bf16[64,1792]{1,0:T(8,128)(2,1)S(1)} %get-tuple-element.45), channel_id=1, source_target_pairs={{0,2},{2,0},{1,3},{3,1},{4,6},{6,4},{5,7},{7,5},{8,10},{10,8},{9,1... | collective-permute-start | bytes 688136 | tf_op jit(solution)/shard_map/ppermute | solution.py:327
  101.6 0.1 add_convert_fusion.2
  101.6 1.5 %collective-permute-done.17 = bf16[64,1792]{1,0:T(8,128)(2,1)S(1)} collective-permute-done((bf16[64,1792]{1,0:T(8,128)(2,1)S(1)}, bf16[64,1792]{1,0:T(8,128)(2,1)S(1)}, u32[]{:S(2)}, u32[]{:S(2)}) %collective-permute-start.17) | collective-permute-done | bytes 229408 | tf_op jit(solution)/shard_map/ppermute | solution.py:327
  103.1 0.7 collective-permute-start.24
  103.8 0.1 add_convert_fusion.3
  103.9 4.1 %collective-permute-done.10 = bf16[64,1792]{1,0:T(8,128)(2,1)S(1)} collective-permute-done((bf16[64,1792]{1,0:T(8,128)(2,1)S(1)}, bf16[64,1792]{1,0:T(8,128)(2,1)S(1)}, u32[]{:S(2)}, u32[]{:S(2)}) %collective-permute-start.10) | collective-permute-done | bytes 229408 | tf_op jit(solution)/shard_map/ppermute | solution.py:327
  108.0 2.6 %collective-permute-start.18 = (bf16[64,1792]{1,0:T(8,128)(2,1)S(1)}, bf16[64,1792]{1,0:T(8,128)(2,1)S(1)}, u32[]{:S(2)}, u32[]{:S(2)}) collective-permute-start(bf16[64,1792]{1,0:T(8,128)(2,1)S(1)} %add_convert_fusion.3), channel_id=1, source_target_pairs={{4,0},{0,4},{12,8},{8,12},{5,1},{1,5},{13,9},{9,13},{6,2},{2,6},{1... | collective-permute-start | bytes 688136 | tf_op jit(solution)/shard_map/ppermute | solution.py:327
  110.7 0.1 add_convert_fusion.4
  110.7 2.2 %collective-permute-done.8 = bf16[64,1792]{1,0:T(8,128)(2,1)S(1)} collective-permute-done((bf16[64,1792]{1,0:T(8,128)(2,1)S(1)}, bf16[64,1792]{1,0:T(8,128)(2,1)S(1)}, u32[]{:S(2)}, u32[]{:S(2)}) %collective-permute-start.8) | collective-permute-done | bytes 229408 | tf_op jit(solution)/shard_map/ppermute | solution.py:327
  112.9 3.1 %collective-permute-start.11 = (bf16[64,1792]{1,0:T(8,128)(2,1)S(1)}, bf16[64,1792]{1,0:T(8,128)(2,1)S(1)}, u32[]{:S(2)}, u32[]{:S(2)}) collective-permute-start(bf16[64,1792]{1,0:T(8,128)(2,1)S(1)} %add_convert_fusion.4), channel_id=1, source_target_pairs={{8,0},{12,4},{0,8},{4,12},{9,1},{13,5},{1,9},{5,13},{10,2},{14,6},... | collective-permute-start | bytes 688136 | tf_op jit(solution)/shard_map/ppermute | solution.py:327
  116.0 0.1 add_convert_fusion.5
  116.1 0.1 collective-permute-start.9
  116.2 0.1 add_convert_fusion.1
  116.2 1.6 %collective-permute-done.12.refs_3_ = bf16[64,1792]{1,0:T(8,128)(2,1)S(1)} collective-permute-done((bf16[64,1792]{1,0:T(8,128)(2,1)S(1)}, bf16[64,1792]{1,0:T(8,128)(2,1)S(1)}, u32[]{:S(2)}, u32[]{:S(2)}) %collective-permute-start.12) | collective-permute-done | bytes 229408 | tf_op jit(solution)/shard_map/ppermute | solution.py:327
  117.8 1.2 collective-permute-start.29
  119.1 3.1 %collective-permute-start.27 = (bf16[64,1792]{1,0:T(8,128)(2,1)S(1)}, bf16[64,1792]{1,0:T(8,128)(2,1)S(1)}, u32[]{:S(2)}, u32[]{:S(2)}) collective-permute-start(bf16[64,1792]{1,0:T(8,128)(2,1)S(1)} %add_convert_fusion.1), channel_id=1, source_target_pairs={{4,0},{0,4},{12,8},{8,12},{5,1},{1,5},{13,9},{9,13},{6,2},{2,6},{1... | collective-permute-start | bytes 688136 | tf_op jit(solution)/shard_map/ppermute | solution.py:327
  122.1 10.2 %collective-permute-done.11.refs_2_ = bf16[64,1792]{1,0:T(8,128)(2,1)S(1)} collective-permute-done((bf16[64,1792]{1,0:T(8,128)(2,1)S(1)}, bf16[64,1792]{1,0:T(8,128)(2,1)S(1)}, u32[]{:S(2)}, u32[]{:S(2)}) %collective-permute-start.11) | collective-permute-done | bytes 229408 | tf_op jit(solution)/shard_map/ppermute | solution.py:327
  132.4 6.7 %collective-permute-done.9.refs_1_ = bf16[64,1792]{1,0:T(8,128)(2,1)S(1)} collective-permute-done((bf16[64,1792]{1,0:T(8,128)(2,1)S(1)}, bf16[64,1792]{1,0:T(8,128)(2,1)S(1)}, u32[]{:S(2)}, u32[]{:S(2)}) %collective-permute-start.9) | collective-permute-done | bytes 229408 | tf_op jit(solution)/shard_map/ppermute | solution.py:327
  139.1 1.4 left.1
  140.5 5.4 %collective-permute-done.29.refs_2_ = bf16[64,1792]{1,0:T(8,128)(2,1)S(1)} collective-permute-done((bf16[64,1792]{1,0:T(8,128)(2,1)S(1)}, bf16[64,1792]{1,0:T(8,128)(2,1)S(1)}, u32[]{:S(2)}, u32[]{:S(2)}) %collective-permute-start.29) | collective-permute-done | bytes 229408 | tf_op jit(solution)/shard_map/ppermute | solution.py:327
  145.9 1.0 right.1
  (14 shorter events, 0.0 us)
Async XLA Ops:
  0.0 54.2 %collective-permute-start.1 = (bf16[3584,512]{1,0:T(8,128)(2,1)}, bf16[3584,512]{1,0:T(8,128)(2,1)}, u32[]{:S(2)}, u32[]{:S(2)}) collective-permute-start(bf16[3584,512]{1,0:T(8,128)(2,1)} %bitcast.9), channel_id=1, source_target_pairs={{0,1},{1,0},{2,3},{3,2},{4,5},{5,4},{6,7},{7,6},{8,9},{9,8},{10,11... | collective-permute-start | bytes 11010056 | tf_op jit(solution)/shard_map/ppermute | solution.py:334
  0.7 54.7 %collective-permute-start.2 = (bf16[3584,512]{1,0:T(8,128)(2,1)}, bf16[3584,512]{1,0:T(8,128)(2,1)}, u32[]{:S(2)}, u32[]{:S(2)}) collective-permute-start(bf16[3584,512]{1,0:T(8,128)(2,1)} %bitcast.11), channel_id=1, source_target_pairs={{0,1},{1,0},{2,3},{3,2},{4,5},{5,4},{6,7},{7,6},{8,9},{9,8},{10,11... | collective-permute-start | bytes 11010056 | tf_op jit(solution)/shard_map/ppermute | solution.py:334
  0.7 55.0 %collective-permute-start.3 = (bf16[512,3584]{1,0:T(8,128)(2,1)}, bf16[512,3584]{1,0:T(8,128)(2,1)}, u32[]{:S(2)}, u32[]{:S(2)}) collective-permute-start(bf16[512,3584]{1,0:T(8,128)(2,1)} %bitcast.13), channel_id=1, source_target_pairs={{0,1},{1,0},{2,3},{3,2},{4,5},{5,4},{6,7},{7,6},{8,9},{9,8},{10,11... | collective-permute-start | bytes 11010056 | tf_op jit(solution)/shard_map/ppermute | solution.py:334
  3.2 17.1 %collective-permute-start.19 = (bf16[64,1792]{1,0:T(8,128)(2,1)S(1)}, bf16[64,1792]{1,0:T(8,128)(2,1)S(1)}, u32[]{:S(2)}, u32[]{:S(2)}) collective-permute-start(bf16[64,1792]{1,0:T(8,128)(2,1)S(1)} %get-tuple-element.50), channel_id=1, source_target_pairs={{0,12},{4,8},{8,4},{12,0},{1,13},{5,9},{9,5},{13,1},{2,14},{6,10},... | collective-permute-start | bytes 688136 | tf_op jit(solution)/shard_map/ppermute | solution.py:327
  4.6 20.6 %collective-permute-start.20 = (bf16[64,1792]{1,0:T(8,128)(2,1)S(1)}, bf16[64,1792]{1,0:T(8,128)(2,1)S(1)}, u32[]{:S(2)}, u32[]{:S(2)}) collective-permute-start(bf16[64,1792]{1,0:T(8,128)(2,1)S(1)} %get-tuple-element.51), channel_id=1, source_target_pairs={{0,12},{4,8},{8,4},{12,0},{1,13},{5,9},{9,5},{13,1},{2,14},{6,10},... | collective-permute-start | bytes 688136 | tf_op jit(solution)/shard_map/ppermute | solution.py:327
  20.3 5.9 %collective-permute-start.13 = (bf16[64,1792]{1,0:T(8,128)(2,1)S(1)}, bf16[64,1792]{1,0:T(8,128)(2,1)S(1)}, u32[]{:S(2)}, u32[]{:S(2)}) collective-permute-start(bf16[64,1792]{1,0:T(8,128)(2,1)S(1)} %get-tuple-element.46), channel_id=1, source_target_pairs={{0,4},{4,0},{8,12},{12,8},{1,5},{5,1},{9,13},{13,9},{2,6},{6,2},{1... | collective-permute-start | bytes 688136 | tf_op jit(solution)/shard_map/ppermute | solution.py:327
  25.2 8.7 %collective-permute-start.14 = (bf16[64,1792]{1,0:T(8,128)(2,1)S(1)}, bf16[64,1792]{1,0:T(8,128)(2,1)S(1)}, u32[]{:S(2)}, u32[]{:S(2)}) collective-permute-start(bf16[64,1792]{1,0:T(8,128)(2,1)S(1)} %get-tuple-element.47), channel_id=1, source_target_pairs={{0,4},{4,0},{8,12},{12,8},{1,5},{5,1},{9,13},{13,9},{2,6},{6,2},{1... | collective-permute-start | bytes 688136 | tf_op jit(solution)/shard_map/ppermute | solution.py:327
  26.1 11.3 %collective-permute-start.4 = (bf16[64,1792]{1,0:T(8,128)(2,1)S(1)}, bf16[64,1792]{1,0:T(8,128)(2,1)S(1)}, u32[]{:S(2)}, u32[]{:S(2)}) collective-permute-start(bf16[64,1792]{1,0:T(8,128)(2,1)S(1)} %get-tuple-element.39), channel_id=1, source_target_pairs={{0,8},{4,12},{8,0},{12,4},{1,9},{5,13},{9,1},{13,5},{2,10},{6,14},... | collective-permute-start | bytes 688136 | tf_op jit(solution)/shard_map/ppermute | solution.py:327
  33.9 12.7 %collective-permute-start.5 = (bf16[64,1792]{1,0:T(8,128)(2,1)S(1)}, bf16[64,1792]{1,0:T(8,128)(2,1)S(1)}, u32[]{:S(2)}, u32[]{:S(2)}) collective-permute-start(bf16[64,1792]{1,0:T(8,128)(2,1)S(1)} %get-tuple-element.40), channel_id=1, source_target_pairs={{0,8},{4,12},{8,0},{12,4},{1,9},{5,13},{9,1},{13,5},{2,10},{6,14},... | collective-permute-start | bytes 688136 | tf_op jit(solution)/shard_map/ppermute | solution.py:327
  37.5 13.6 %collective-permute-start.21 = (bf16[64,1792]{1,0:T(8,128)(2,1)S(1)}, bf16[64,1792]{1,0:T(8,128)(2,1)S(1)}, u32[]{:S(2)}, u32[]{:S(2)}) collective-permute-start(bf16[64,1792]{1,0:T(8,128)(2,1)S(1)} %collective-permute-done.19.refs_0_), channel_id=1, source_target_pairs={{0,2},{2,0},{1,3},{3,1},{4,6},{6,4},{5,7},{7,5},{8,10},{10,8},{9,1... | collective-permute-start | bytes 688136 | tf_op jit(solution)/shard_map/ppermute | solution.py:327
  46.6 7.3 %collective-permute-start.22 = (bf16[64,1792]{1,0:T(8,128)(2,1)S(1)}, bf16[64,1792]{1,0:T(8,128)(2,1)S(1)}, u32[]{:S(2)}, u32[]{:S(2)}) collective-permute-start(bf16[64,1792]{1,0:T(8,128)(2,1)S(1)} %collective-permute-done.20.refs_1_), channel_id=1, source_target_pairs={{0,2},{2,0},{1,3},{3,1},{4,6},{6,4},{5,7},{7,5},{8,10},{10,8},{9,1... | collective-permute-start | bytes 688136 | tf_op jit(solution)/shard_map/ppermute | solution.py:327
  51.1 39.7 %collective-permute-start = (bf16[64,3584]{1,0:T(8,128)(2,1)S(1)}, bf16[64,3584]{1,0:T(8,128)(2,1)S(1)}, u32[]{:S(2)}, u32[]{:S(2)}) collective-permute-start(bf16[64,3584]{1,0:T(8,128)(2,1)S(1)} %get-tuple-element.34.refs_0_), channel_id=1, source_target_pairs={{0,2},{2,0},{1,3},{3,1},{4,6},{6,4},{5,7},{7,5},{8,10},{10,8},{9,1... | collective-permute-start | bytes 1376264 | tf_op jit(solution)/shard_map/ppermute | solution.py:327
  53.9 14.7 %collective-permute-start.15 = (bf16[64,1792]{1,0:T(8,128)(2,1)S(1)}, bf16[64,1792]{1,0:T(8,128)(2,1)S(1)}, u32[]{:S(2)}, u32[]{:S(2)}) collective-permute-start(bf16[64,1792]{1,0:T(8,128)(2,1)S(1)} %collective-permute-done.13.refs_0_), channel_id=1, source_target_pairs={{0,2},{2,0},{1,3},{3,1},{4,6},{6,4},{5,7},{7,5},{8,10},{10,8},{9,1... | collective-permute-start | bytes 688136 | tf_op jit(solution)/shard_map/ppermute | solution.py:327
  54.2 19.4 %collective-permute-start.16 = (bf16[64,1792]{1,0:T(8,128)(2,1)S(1)}, bf16[64,1792]{1,0:T(8,128)(2,1)S(1)}, u32[]{:S(2)}, u32[]{:S(2)}) collective-permute-start(bf16[64,1792]{1,0:T(8,128)(2,1)S(1)} %collective-permute-done.14.refs_1_), channel_id=1, source_target_pairs={{0,2},{2,0},{1,3},{3,1},{4,6},{6,4},{5,7},{7,5},{8,10},{10,8},{9,1... | collective-permute-start | bytes 688136 | tf_op jit(solution)/shard_map/ppermute | solution.py:327
  55.4 25.6 %collective-permute-start.6 = (bf16[64,1792]{1,0:T(8,128)(2,1)S(1)}, bf16[64,1792]{1,0:T(8,128)(2,1)S(1)}, u32[]{:S(2)}, u32[]{:S(2)}) collective-permute-start(bf16[64,1792]{1,0:T(8,128)(2,1)S(1)} %collective-permute-done.4.refs_0_), channel_id=1, source_target_pairs={{0,2},{2,0},{1,3},{3,1},{4,6},{6,4},{5,7},{7,5},{8,10},{10,8},{9,1... | collective-permute-start | bytes 688136 | tf_op jit(solution)/shard_map/ppermute | solution.py:327
  55.6 27.8 %collective-permute-start.7 = (bf16[64,1792]{1,0:T(8,128)(2,1)S(1)}, bf16[64,1792]{1,0:T(8,128)(2,1)S(1)}, u32[]{:S(2)}, u32[]{:S(2)}) collective-permute-start(bf16[64,1792]{1,0:T(8,128)(2,1)S(1)} %collective-permute-done.5.refs_1_), channel_id=1, source_target_pairs={{0,2},{2,0},{1,3},{3,1},{4,6},{6,4},{5,7},{7,5},{8,10},{10,8},{9,1... | collective-permute-start | bytes 688136 | tf_op jit(solution)/shard_map/ppermute | solution.py:327
  68.7 31.2 %collective-permute-start.28 = (bf16[64,1792]{1,0:T(8,128)(2,1)S(1)}, bf16[64,1792]{1,0:T(8,128)(2,1)S(1)}, u32[]{:S(2)}, u32[]{:S(2)}) collective-permute-start(bf16[64,1792]{1,0:T(8,128)(2,1)S(1)} %get-tuple-element.61), channel_id=1, source_target_pairs={{0,2},{2,0},{1,3},{3,1},{4,6},{6,4},{5,7},{7,5},{8,10},{10,8},{9,1... | collective-permute-start | bytes 688136 | tf_op jit(solution)/shard_map/ppermute | solution.py:327
  80.9 35.1 %collective-permute-start.26 = (bf16[64,1792]{1,0:T(8,128)(2,1)S(1)}, bf16[64,1792]{1,0:T(8,128)(2,1)S(1)}, u32[]{:S(2)}, u32[]{:S(2)}) collective-permute-start(bf16[64,1792]{1,0:T(8,128)(2,1)S(1)} %get-tuple-element.59), channel_id=1, source_target_pairs={{0,2},{2,0},{1,3},{3,1},{4,6},{6,4},{5,7},{7,5},{8,10},{10,8},{9,1... | collective-permute-start | bytes 688136 | tf_op jit(solution)/shard_map/ppermute | solution.py:327
  81.0 19.0 %collective-permute-start.23 = (bf16[64,1792]{1,0:T(8,128)(2,1)S(1)}, bf16[64,1792]{1,0:T(8,128)(2,1)S(1)}, u32[]{:S(2)}, u32[]{:S(2)}) collective-permute-start(bf16[64,1792]{1,0:T(8,128)(2,1)S(1)} %get-tuple-element.53), channel_id=1, source_target_pairs={{0,2},{2,0},{1,3},{3,1},{4,6},{6,4},{5,7},{7,5},{8,10},{10,8},{9,1... | collective-permute-start | bytes 688136 | tf_op jit(solution)/shard_map/ppermute | solution.py:327
  83.4 19.7 %collective-permute-start.17 = (bf16[64,1792]{1,0:T(8,128)(2,1)S(1)}, bf16[64,1792]{1,0:T(8,128)(2,1)S(1)}, u32[]{:S(2)}, u32[]{:S(2)}) collective-permute-start(bf16[64,1792]{1,0:T(8,128)(2,1)S(1)} %get-tuple-element.49), channel_id=1, source_target_pairs={{0,2},{2,0},{1,3},{3,1},{4,6},{6,4},{5,7},{7,5},{8,10},{10,8},{9,1... | collective-permute-start | bytes 688136 | tf_op jit(solution)/shard_map/ppermute | solution.py:327
  90.8 17.2 %collective-permute-start.10 = (bf16[64,1792]{1,0:T(8,128)(2,1)S(1)}, bf16[64,1792]{1,0:T(8,128)(2,1)S(1)}, u32[]{:S(2)}, u32[]{:S(2)}) collective-permute-start(bf16[64,1792]{1,0:T(8,128)(2,1)S(1)} %get-tuple-element.44), channel_id=1, source_target_pairs={{0,2},{2,0},{1,3},{3,1},{4,6},{6,4},{5,7},{7,5},{8,10},{10,8},{9,1... | collective-permute-start | bytes 688136 | tf_op jit(solution)/shard_map/ppermute | solution.py:327
  99.9 39.2 %copy-start = (s32[128,1]{0,1:T(1,128)S(1)}, s32[128,1]{0,1:T(1,128)}, u32[]{:S(2)}) copy-start(s32[128,1]{0,1:T(1,128)} %param.7) | copy-start | bytes 1540
  99.9 39.2 %copy-start.1 = (f32[128,1]{0,1:T(1,128)S(1)}, f32[128,1]{0,1:T(1,128)}, u32[]{:S(2)}) copy-start(f32[128,1]{0,1:T(1,128)} %param.8) | copy-start | bytes 1540
  99.9 13.0 %collective-permute-start.8 = (bf16[64,1792]{1,0:T(8,128)(2,1)S(1)}, bf16[64,1792]{1,0:T(8,128)(2,1)S(1)}, u32[]{:S(2)}, u32[]{:S(2)}) collective-permute-start(bf16[64,1792]{1,0:T(8,128)(2,1)S(1)} %get-tuple-element.42), channel_id=1, source_target_pairs={{0,2},{2,0},{1,3},{3,1},{4,6},{6,4},{5,7},{7,5},{8,10},{10,8},{9,1... | collective-permute-start | bytes 688136 | tf_op jit(solution)/shard_map/ppermute | solution.py:327
  100.0 17.8 %collective-permute-start.12 = (bf16[64,1792]{1,0:T(8,128)(2,1)S(1)}, bf16[64,1792]{1,0:T(8,128)(2,1)S(1)}, u32[]{:S(2)}, u32[]{:S(2)}) collective-permute-start(bf16[64,1792]{1,0:T(8,128)(2,1)S(1)} %get-tuple-element.45), channel_id=1, source_target_pairs={{0,2},{2,0},{1,3},{3,1},{4,6},{6,4},{5,7},{7,5},{8,10},{10,8},{9,1... | collective-permute-start | bytes 688136 | tf_op jit(solution)/shard_map/ppermute | solution.py:327
  103.1 14.8 %collective-permute-start.24 = (bf16[64,1792]{1,0:T(8,128)(2,1)S(1)}, bf16[64,1792]{1,0:T(8,128)(2,1)S(1)}, u32[]{:S(2)}, u32[]{:S(2)}) collective-permute-start(bf16[64,1792]{1,0:T(8,128)(2,1)S(1)} %add_convert_fusion.2), channel_id=1, source_target_pairs={{12,0},{8,4},{4,8},{0,12},{13,1},{9,5},{5,9},{1,13},{14,2},{10,6},... | collective-permute-start | bytes 688136 | tf_op jit(solution)/shard_map/ppermute | solution.py:327
  108.0 11.1 %collective-permute-start.18 = (bf16[64,1792]{1,0:T(8,128)(2,1)S(1)}, bf16[64,1792]{1,0:T(8,128)(2,1)S(1)}, u32[]{:S(2)}, u32[]{:S(2)}) collective-permute-start(bf16[64,1792]{1,0:T(8,128)(2,1)S(1)} %add_convert_fusion.3), channel_id=1, source_target_pairs={{4,0},{0,4},{12,8},{8,12},{5,1},{1,5},{13,9},{9,13},{6,2},{2,6},{1... | collective-permute-start | bytes 688136 | tf_op jit(solution)/shard_map/ppermute | solution.py:327
  112.9 19.5 %collective-permute-start.11 = (bf16[64,1792]{1,0:T(8,128)(2,1)S(1)}, bf16[64,1792]{1,0:T(8,128)(2,1)S(1)}, u32[]{:S(2)}, u32[]{:S(2)}) collective-permute-start(bf16[64,1792]{1,0:T(8,128)(2,1)S(1)} %add_convert_fusion.4), channel_id=1, source_target_pairs={{8,0},{12,4},{0,8},{4,12},{9,1},{13,5},{1,9},{5,13},{10,2},{14,6},... | collective-permute-start | bytes 688136 | tf_op jit(solution)/shard_map/ppermute | solution.py:327
  116.1 23.0 %collective-permute-start.9 = (bf16[64,1792]{1,0:T(8,128)(2,1)S(1)}, bf16[64,1792]{1,0:T(8,128)(2,1)S(1)}, u32[]{:S(2)}, u32[]{:S(2)}) collective-permute-start(bf16[64,1792]{1,0:T(8,128)(2,1)S(1)} %add_convert_fusion.5), channel_id=1, source_target_pairs={{8,0},{12,4},{0,8},{4,12},{9,1},{13,5},{1,9},{5,13},{10,2},{14,6},... | collective-permute-start | bytes 688136 | tf_op jit(solution)/shard_map/ppermute | solution.py:327
  117.8 22.7 %collective-permute-start.25 = (bf16[64,1792]{1,0:T(8,128)(2,1)S(1)}, bf16[64,1792]{1,0:T(8,128)(2,1)S(1)}, u32[]{:S(2)}, u32[]{:S(2)}) collective-permute-start(bf16[64,1792]{1,0:T(8,128)(2,1)S(1)} %get-tuple-element.57), channel_id=1, source_target_pairs={{0,2},{2,0},{1,3},{3,1},{4,6},{6,4},{5,7},{7,5},{8,10},{10,8},{9,1... | collective-permute-start | bytes 688136 | tf_op jit(solution)/shard_map/ppermute | solution.py:327
  117.8 28.0 %collective-permute-start.29 = (bf16[64,1792]{1,0:T(8,128)(2,1)S(1)}, bf16[64,1792]{1,0:T(8,128)(2,1)S(1)}, u32[]{:S(2)}, u32[]{:S(2)}) collective-permute-start(bf16[64,1792]{1,0:T(8,128)(2,1)S(1)} %add_convert_fusion), channel_id=1, source_target_pairs={{12,0},{8,4},{4,8},{0,12},{13,1},{9,5},{5,9},{1,13},{14,2},{10,6},... | collective-permute-start | bytes 688136 | tf_op jit(solution)/shard_map/ppermute | solution.py:327
  119.1 26.8 %collective-permute-start.27 = (bf16[64,1792]{1,0:T(8,128)(2,1)S(1)}, bf16[64,1792]{1,0:T(8,128)(2,1)S(1)}, u32[]{:S(2)}, u32[]{:S(2)}) collective-permute-start(bf16[64,1792]{1,0:T(8,128)(2,1)S(1)} %add_convert_fusion.1), channel_id=1, source_target_pairs={{4,0},{0,4},{12,8},{8,12},{5,1},{1,5},{13,9},{9,13},{6,2},{2,6},{1... | collective-permute-start | bytes 688136 | tf_op jit(solution)/shard_map/ppermute | solution.py:327
